TPU v7x, 32 devices: a whole 2x2x4 slice. The times are simulated.
32 devices in a mesh: dp: 8 (over z, x), segment: 2 (over y), mp: 2 (over core).
Axes of the slice: x: 2, y: 2, z: 4, core: 2. Of those that a mesh axis runs over, the one named last changes fastest.
Arguments:
- prefix_hidden: bfloat16 [16, 512, 8192], P(('dp', 'segment'), 'mp'), may hold values from -6 to 6
- norm_gain: float32 [8192], replicated, may hold values from 0.5 to 1.5
- kv_weight: bfloat16 [8192, 2, 1024], P('dp', None, 'mp'), may hold values from -0.0625 to 0.0625
- action_query: bfloat16 [16, 128, 2048], P(('dp', 'segment'), None, 'mp'), may hold values from -104 to 104
- action_kv: bfloat16 [16, 128, 2, 1024], P(('dp', 'segment'), None, None, 'mp'), may hold values from -4.25 to 4.25
- out_cotangent: bfloat16 [16, 128, 2048], P(('dp', 'segment'), None, 'mp'), may hold values from -18 to 18
- prefix_blocks: int32 [16, 512], P(('dp', 'segment')), may hold values from 0 to 7, as said below
- action_blocks: int32 [16, 128], P(('dp', 'segment')), may hold values from 0 to 8, as said below
- prefix_lengths: int32 [16], P(('dp', 'segment')), may hold values from 128 to 512, as said below
- timesteps: int32 [16], P(('dp', 'segment')), may hold values from 0 to 999
Outputs:
- attn_out: bfloat16 [16, 128, 2048], P(('dp', 'segment'), None, 'mp')
- query_grad: float32 [16, 128, 2048], P(('dp', 'segment'), None, 'mp')
- action_kv_grad: float32 [16, 128, 2, 1024], P(('dp', 'segment'), None, None, 'mp')
- weight_grad: float32 [8192, 2, 1024], P('dp', None, 'mp')
Inputs may be any that keep to these rules, and one draw needn't show every extreme that they name: `prefix_blocks`: constant over each run of 64 positions, 0 on the first run, rising by 0 or 1 from one run to the next; in every draw some sample rises at every run. `action_blocks`: constant over each run of 64 positions; the last run of every sample holds 8; in every draw some sample's first run holds 0. `prefix_lengths`: in every draw some sample's prefix is whole and some sample's is 128.
All inputs are finite; a program needn't handle non-finite values.
Results may differ from a plain program's by a relative error of at most 0.017.
Values may be sent and summed in bfloat16 or wider, within the bound.
A program may use at most 128 MiB of HBM per device.

v0:
```python
import jax
import jax.numpy as jnp
from jax import lax
from jax.sharding import PartitionSpec as P

KVH = 8
HD = 128
QH = 16
STEPS = 1000


EPS = 1e-06
NEGATIVE = -1e30


def head_scores(query, keys):
    return jnp.einsum("agrh,jgh->graj", query, keys, preferred_element_type=jnp.float32) * HD ** (
        -0.5
    )


def backward_terms(probs, values, keys, query, grad_out):
    probs_low = probs.astype(jnp.bfloat16)
    d_probs = jnp.einsum("agrh,jgh->graj", grad_out, values, preferred_element_type=jnp.float32)
    delta = jnp.sum(probs * d_probs, axis=-1, keepdims=True)
    d_scores = (probs * (d_probs - delta)).astype(jnp.bfloat16)
    d_query = jnp.einsum(
        "graj,jgh->agrh", d_scores, keys, preferred_element_type=jnp.float32
    ) * HD ** (-0.5)
    d_keys = jnp.einsum(
        "graj,agrh->jgh", d_scores, query, preferred_element_type=jnp.float32
    ) * HD ** (-0.5)
    d_values = jnp.einsum("graj,agrh->jgh", probs_low, grad_out, preferred_element_type=jnp.float32)
    return (d_query, jnp.stack([d_keys, d_values], axis=1))


def shards(
    prefix_hidden,
    norm_gain,
    kv_weight,
    action_query,
    action_kv,
    out_cotangent,
    prefix_blocks,
    action_blocks,
    prefix_lengths,
    timesteps,
):
    acts = action_query.shape[1]
    heads_kv = kv_weight.shape[2] // HD
    ratio = QH // KVH
    columns = 2 * kv_weight.shape[2]
    wide = prefix_hidden[0].astype(jnp.float32)
    inverse = lax.rsqrt(jnp.mean(wide * wide, axis=-1, keepdims=True) + EPS)
    normed_local = (wide * inverse * norm_gain).astype(jnp.bfloat16)
    normed = lax.all_gather(normed_local, "mp", axis=0, tiled=True)
    rows = normed.shape[0]
    piece = lax.all_gather(kv_weight, "dp", axis=0, tiled=True)
    section = normed
    projected = jnp.dot(
        section, piece.reshape(piece.shape[0], columns), preferred_element_type=jnp.float32
    )
    prefix_kv = projected.astype(jnp.bfloat16).reshape(rows, 2, heads_kv, HD)
    own_pair = action_kv[0].reshape(acts, 2, heads_kv, HD)
    query = action_query[0].reshape(acts, heads_kv, ratio, HD)
    flow_weight = 0.5 + (timesteps[0].astype(jnp.float32) + 0.5) / STEPS
    grad_out = (
        (flow_weight * out_cotangent[0].astype(jnp.float32))
        .astype(jnp.bfloat16)
        .reshape(acts, heads_kv, ratio, HD)
    )
    pblocks = prefix_blocks[0]
    ablocks = action_blocks[0]
    length = prefix_lengths[0]
    keys = jnp.concatenate([prefix_kv[:, 0], own_pair[:, 0]], axis=0)
    values = jnp.concatenate([prefix_kv[:, 1], own_pair[:, 1]], axis=0)
    positions = jnp.arange(rows, dtype=jnp.int32)
    see_prefix = (pblocks[None, :] <= ablocks[:, None]) & (positions[None, :] < length)
    see_action = ablocks[None, :] <= ablocks[:, None]
    visible = jnp.concatenate([see_prefix, see_action], axis=1)
    masked = jnp.where(visible, head_scores(query, keys), NEGATIVE)
    top = jnp.max(masked, axis=-1, keepdims=True)
    expo = jnp.where(visible, jnp.exp(masked - top), 0.0)
    probs = expo / jnp.sum(expo, axis=-1, keepdims=True)
    out = jnp.einsum(
        "graj,jgh->agrh", probs.astype(jnp.bfloat16), values, preferred_element_type=jnp.float32
    )
    d_query, d_pair = backward_terms(probs, values, keys, query, grad_out)
    d_prefix = d_pair[:rows]
    d_action = d_pair[rows:]
    attn_out = out.astype(jnp.bfloat16).reshape(1, acts, ratio * heads_kv * HD)
    query_grad = d_query.reshape(1, acts, ratio * heads_kv * HD)
    action_kv_grad = d_action.reshape(1, acts, 2, heads_kv * HD)
    prefix_grad = d_prefix.astype(jnp.bfloat16).reshape(rows, columns)
    section = normed
    term = lax.dot_general(
        section, prefix_grad, (((0,), (0,)), ((), ())), preferred_element_type=jnp.float32
    )
    shard = lax.psum_scatter(
        term.reshape(kv_weight.shape[0] * lax.axis_size("dp"), 2, columns // 2).astype(
            jnp.bfloat16
        ),
        "dp",
        scatter_dimension=0,
        tiled=True,
    )
    weight_grad = lax.psum(shard, "segment").astype(jnp.float32)
    return (attn_out, query_grad, action_kv_grad, weight_grad)


def solution(mesh):
    placed = (
        P(("dp", "segment"), "mp", None),
        P(),
        P("dp", None, "mp"),
        P(("dp", "segment"), None, "mp"),
        P(("dp", "segment"), None, None, "mp"),
        P(("dp", "segment"), None, "mp"),
        P(("dp", "segment"), None),
        P(("dp", "segment"), None),
        P(("dp", "segment")),
        P(("dp", "segment")),
    )
    return jax.shard_map(
        shards,
        mesh=mesh,
        in_specs=placed,
        out_specs=(
            P(("dp", "segment"), None, "mp"),
            P(("dp", "segment"), None, "mp"),
            P(("dp", "segment"), None, None, "mp"),
            P("dp", None, "mp"),
        ),
        check_vma=False,
    )
```

profile of v0, /device:TPU:0, one launch (start us, length us, event | category | flops | bytes accessed | tf_op | source)
XLA Modules:
  0.0 657.0 jit_solution(16205726771575805277)
XLA Ops:
  7.2 0.0 all-gather.5.cloned.1.call-start
  7.2 0.7 all-gather.5.cloned.1.call-update
  7.9 0.0 all-gather.3.cloned.1.call-start
  8.0 6.4 copy.51
  14.3 3.5 fusion.1
  17.8 2.6 fusion.3
  20.5 0.0 copy-start.11
  20.5 0.0 all-gather.3.cloned.1.call-update
  20.5 0.0 reduce-scatter.2.cloned.1.call-start
  22.0 0.8 copy.88
  22.9 0.2 copy.87
  23.1 0.2 copy.53
  23.3 0.7 fusion.29
  24.0 0.1 copy.86
  24.1 0.1 broadcast_compare_fusion
  24.2 0.2 compare_and_fusion
  24.4 0.6 pad_add_fusion
  25.1 215.0 %all-gather.5.cloned.1.call-done = bf16[8192,2,512]{2,1,0:T(2,128)(2,1)} async-done(((bf16[1024,2,512]{2,1,0:T(2,128)(2,1)}), bf16[8192,2,512]{2,1,0:T(2,128)(2,1)}) %all-gather.5.cloned.1.call-update) | async-done | bytes 16777232 | tf_op jit(solution)/shard_map/all_gather | solution.py:58
  240.1 17.3 %copy.89 = bf16[1024,8,2,512]{3,1,2,0:T(8,128)(2,1)} copy(bf16[1024,8,2,512]{3,2,1,0:T(2,128)(2,1)} %bitcast.107) | data formatting | bytes 33554432
  257.5 1.1 all-gather.3.cloned.1.call-done
  258.5 14.8 %convolution_convert_fusion.1 = bf16[512,1024]{1,0:T(8,128)(2,1)S(1)} fusion(bf16[512,8192]{0,1:T(8,128)(2,1)} %all-gather.3.cloned.1.call-done, bf16[8192,1024]{1,0:T(8,128)(2,1)} %bitcast.108), kind=kOutput, calls=%fused_computation.20 | convolution fusion | flops 8590458880 | bytes 26214400 | tf_op jit(solution)/shard_map/dot_general | solution.py:60
  273.4 0.8 reshape.62
  274.2 0.4 fusion.28
  274.5 0.1 copy.91
  274.6 1.1 copy.84
  275.7 2.1 fusion.30
  277.9 0.0 copy-start.3
  277.9 0.0 copy-start.8
  277.9 1.8 convolution_bitcast_fusion
  279.7 0.1 copy-done.7
  279.8 0.1 copy-done.8
  279.9 0.6 fusion.5
  280.5 2.2 fusion.7
  282.7 0.5 fusion.11
  283.3 0.2 fusion.8
  283.4 16.1 %convolution_convert_fusion = bf16[8192,2,512]{2,0,1:T(8,128)(2,1)} fusion(bf16[2,512,512]{2,1,0:T(8,128)(2,1)S(1)} %bitcast.113, bf16[512,8192]{0,1:T(8,128)(2,1)} %all-gather.3.cloned.1.call-done), kind=kOutput, calls=%fused_computation.1 | convolution fusion | flops 8598323200 | bytes 26214400 | tf_op jit(solution)/shard_map/dot_general | solution.py:96
  299.5 0.0 reduce-scatter.2.cloned.1.call-update
  299.5 0.0 all-reduce.2.cloned.1.call-start
  299.6 280.8 %reduce-scatter.2.cloned.1.call-done = bf16[1024,2,512]{2,0,1:T(8,128)(2,1)} async-done(((bf16[8192,2,512]{2,0,1:T(8,128)(2,1)}), bf16[1024,2,512]{2,0,1:T(8,128)(2,1)}) %reduce-scatter.2.cloned.1.call-update) | async-done | bytes 2097168 | tf_op jit(solution)/shard_map/reduce_scatter | solution.py:99
  580.4 0.0 all-reduce.2.cloned.1.call-update
  580.5 2.3 convolution_convert_fusion.2
  582.8 0.9 copy.66
  583.6 1.2 convolution_multiply_fusion
  584.9 2.0 copy.67
  586.9 1.0 fusion.17
  588.0 1.0 copy.68
  589.0 55.8 %all-reduce.2.cloned.1.call-done = bf16[1024,2,512]{2,0,1:T(8,128)(2,1)} async-done(((bf16[1024,2,512]{2,0,1:T(8,128)(2,1)}), bf16[1024,2,512]{2,0,1:T(8,128)(2,1)}) %all-reduce.2.cloned.1.call-update) | async-done | bytes 2097168 | tf_op jit(solution)/shard_map/psum | solution.py:107
  644.7 5.8 copy.69
  (22 shorter events, 0.1 us)
Async XLA Ops:
  7.2 233.0 %all-gather.5.cloned.1.call-start = ((), (), s32[]{:S(2)}) async-start(), calls=%async_computation.2 | async-start | bytes 18874368 | tf_op jit(solution)/shard_map/all_gather | solution.py:58
  7.9 250.6 %all-gather.3.cloned.1.call-start = ((), (), s32[]{:S(2)}) async-start(), calls=%async_computation.1 | async-start | bytes 12582912 | tf_op jit(solution)/shard_map/all_gather | solution.py:56
  7.9 9.8 %copy-start.9 = (f32[8192]{0:T(1024)S(1)}, f32[8192]{0:T(1024)}, u32[]{:S(2)}) copy-start(f32[8192]{0:T(1024)} %param.11) | copy-start | bytes 98308
  14.3 3.5 copy-start
  20.4 1.5 copy-start.4
  20.4 2.4 copy-start.5
  20.4 2.6 copy-start.6
  20.4 3.7 copy-start.10
  20.5 3.8 copy-start.11
  20.5 559.9 %reduce-scatter.2.cloned.1.call-start = ((), (), s32[]{:S(2)}) async-start(), calls=%async_computation.3 | async-start | bytes 18874368 | tf_op jit(solution)/shard_map/reduce_scatter | solution.py:99
  277.9 1.9 copy-start.2
  277.9 1.9 copy-start.3
  277.9 1.9 copy-start.7
  277.9 2.0 copy-start.8
  279.7 3.5 copy-start.1
  299.5 345.2 %all-reduce.2.cloned.1.call-start = ((), (), s32[]{:S(2)}) async-start(), calls=%async_computation.4 | async-start | bytes 4194304 | tf_op jit(solution)/shard_map/psum | solution.py:107
Sparse Core Ops, SparseCore 0:
  10.1 229.9 all-gather.4
  242.2 16.2 all-gather.2
  299.7 280.7 reduce-scatter.1
  582.6 62.1 all-reduce.1
where the time goes:
time: 658 us; the launch traced here: 657 us
  waiting for transfers between devices  553 us (84%)
  matrix products  39.5 us (6%)
  local copies, waits for them, and re-layouts  38 us (6%)
  between operations  15.4 us (2%)
  other arithmetic  10.5 us (2%)
    reduce_scatter x1, waiting for transfers between devices, shards(): lax.psum_scatter(term.reshape(kv_weight.shape[0] * lax.axis_size('dp'), 2...  281 us
    all_gather x1, waiting for transfers between devices, shards(): piece = lax.all_gather(kv_weight, 'dp', axis=0, tiled=True)  215 us
    psum x1, waiting for transfers between devices, shards(): weight_grad = lax.psum(shard, 'segment').astype(jnp.float32)  55.8 us
    unnamed x34, local copies, waits for them, and re-layouts  35.1 us
    dot_general x1, matrix products, shards(): lax.dot_general(section, prefix_grad, (((0,), (0,)), ((), ())), preferred...  16.1 us
    dot_general x1, matrix products, shards(): jnp.dot(section, piece.reshape(piece.shape[0], columns), preferred_elemen...  14.8 us
  transfers between devices with their start and end apart: 4, of which 4 were waited for; matrix products, arithmetic and copies ran while one was open for 6% of the time, Pallas kernels for 0%

commit v1 on v0

v1 whole, which is shorter than its diff:
```python
import functools

import jax
import jax.numpy as jnp
from jax import lax
from jax.experimental import pallas as pl
from jax.experimental.pallas import tpu as pltpu
from jax.sharding import PartitionSpec as P

KVH = 8
HD = 128
QH = 16
STEPS = 1000


EPS = 1e-06
NEGATIVE = -1e30
CHUNKS = 4
MiB = 1 << 20


def inner_of(ndp):
    return 2 if ndp % 2 == 0 else 1


def remote(src, dst, send_sem, recv_sem, where):
    return pltpu.make_async_remote_copy(
        src_ref=src,
        dst_ref=dst,
        send_sem=send_sem,
        recv_sem=recv_sem,
        device_id=where,
        device_id_type=pl.DeviceIdType.MESH,
    )


def greet(peers):
    barrier = pltpu.get_barrier_semaphore()
    for peer in peers:
        pl.semaphore_signal(
            barrier, inc=1, device_id=peer, device_id_type=pl.DeviceIdType.MESH
        )
    pl.semaphore_wait(barrier, len(peers))


def gather_kernel(
    ndp, nmp, w_ref, n_ref, w_all, n_all,
    own_sem, zs, zr, xs, xr, ys, yr, ms, mr, fs, fr,
):
    nx = inner_of(ndp)
    nz = ndp // nx
    dp, seg, mp = lax.axis_index("dp"), lax.axis_index("segment"), lax.axis_index("mp")
    z, x = dp // nx, dp % nx
    z_peer = [{"dp": ((z + o) % nz) * nx + x} for o in range(1, nz)]
    x_peer = {"dp": z * nx + (nx - 1 - x)}
    y_peer = {"segment": 1 - seg}
    m_peer = [{"mp": (mp + o) % nmp} for o in range(1, nmp)]
    greet(z_peer + ([x_peer] if nx > 1 else []) + [y_peer] + m_peer)
    rows = n_ref.shape[0] // CHUNKS

    own_w = pltpu.make_async_copy(w_ref, w_all.at[dp], own_sem.at[0])
    own_n = pltpu.make_async_copy(n_ref, n_all.at[seg, mp], own_sem.at[1])
    started = []
    order = sorted(range(1, nz), key=lambda o: min(o, nz - o))
    z_copy = {o: remote(w_ref, w_all.at[dp], zs.at[o - 1], zr.at[o - 1], z_peer[o - 1]) for o in order}
    y_copy = [
        remote(
            n_ref.at[pl.ds(c * rows, rows)],
            n_all.at[seg, mp, pl.ds(c * rows, rows)],
            ys.at[c], yr.at[c], y_peer,
        )
        for c in range(CHUNKS)
    ]
    x_copy = []
    if nx > 1:
        x_copy.append(remote(w_ref, w_all.at[dp], xs.at[0], xr.at[0], x_peer))
    m_copy = [remote(n_ref, n_all.at[seg, mp], ms.at[o], mr.at[o], m_peer[o]) for o in range(nmp - 1)]
    for copy in list(z_copy.values()) + x_copy + y_copy + m_copy + [own_w, own_n]:
        copy.start()
    f_copy = []

    def on_z(o):
        z_copy[o].wait_recv()
        if nx > 1:
            src = ((z + nz - o) % nz) * nx + x
            copy = remote(w_all.at[src], w_all.at[src], xs.at[o], xr.at[o], x_peer)
            copy.start()
            x_copy.append(copy)

    def on_y(c):
        y_copy[c].wait_recv()
        for o in range(nmp - 1):
            part = n_all.at[1 - seg, mp, pl.ds(c * rows, rows)]
            copy = remote(part, part, fs.at[o, c], fr.at[o, c], m_peer[o])
            copy.start()
            f_copy.append(copy)

    for i in range(max(len(order), CHUNKS)):
        if i < len(order):
            on_z(order[i])
        if i < CHUNKS:
            on_y(i)
    own_w.wait()
    own_n.wait()
    for copy in m_copy + x_copy + f_copy:
        copy.wait_recv()
    for copy in list(z_copy.values()) + y_copy + m_copy + x_copy + f_copy:
        copy.wait_send()


def gather(ndp, nseg, nmp, weight, normed):
    nx = inner_of(ndp)
    nz = ndp // nx
    dma = pltpu.SemaphoreType.DMA
    vmem = pl.BlockSpec(memory_space=pltpu.VMEM)
    anys = pl.BlockSpec(memory_space=pl.ANY)
    return pl.pallas_call(
        functools.partial(gather_kernel, ndp, nmp),
        out_shape=(
            jax.ShapeDtypeStruct((ndp,) + weight.shape, weight.dtype),
            jax.ShapeDtypeStruct((nseg, nmp) + normed.shape, normed.dtype),
        ),
        in_specs=[vmem, vmem],
        out_specs=(anys, anys),
        scratch_shapes=[
            dma((2,)),
            dma((max(nz - 1, 1),)), dma((max(nz - 1, 1),)),
            dma((nz,)), dma((nz,)),
            dma((CHUNKS,)), dma((CHUNKS,)),
            dma((max(nmp - 1, 1),)), dma((max(nmp - 1, 1),)),
            dma((max(nmp - 1, 1), CHUNKS)), dma((max(nmp - 1, 1), CHUNKS)),
        ],
        compiler_params=pltpu.CompilerParams(
            collective_id=0, has_side_effects=True, vmem_limit_bytes=16 * MiB
        ),
        name="gather",
    )(weight, normed)


def attention_kernel(
    heads, ratio, kvc, q_ref, akv_ref, go_ref, vis_ref,
    out_ref, dq_ref, dakv_ref, g_ref, pair, grad, sems,
):
    seg = lax.axis_index("segment")
    peer = {"segment": 1 - seg}
    greet([peer])
    give = remote(kvc.at[1 - seg], pair.at[seg], sems.at[0], sems.at[1], peer)
    give.start()
    keep = pltpu.make_async_copy(kvc.at[seg], pair.at[seg], sems.at[2])
    keep.start()
    keep.wait()
    give.wait()
    acts = q_ref.shape[0]
    rows = pair.shape[1]
    scale = HD ** (-0.5)
    vis = vis_ref[...]
    visible = jnp.concatenate([vis] * ratio, axis=0) > 0.5

    def dot(a, b, ca, cb):
        return lax.dot_general(a, b, (((ca,), (cb,)), ((), ())), preferred_element_type=jnp.float32)

    for g in range(heads):
        cols = slice(g * HD, (g + 1) * HD)
        keys = jnp.concatenate([pair[0, :, cols], akv_ref[0, :, cols]], axis=0)
        values = jnp.concatenate([pair[1, :, cols], akv_ref[1, :, cols]], axis=0)
        hs = [slice((g * ratio + r) * HD, (g * ratio + r + 1) * HD) for r in range(ratio)]
        query = jnp.concatenate([q_ref[:, h] for h in hs], axis=0)
        go = jnp.concatenate([go_ref[:, h] for h in hs], axis=0)
        masked = jnp.where(visible, dot(query, keys, 1, 1) * scale, NEGATIVE)
        top = jnp.max(masked, axis=-1, keepdims=True)
        expo = jnp.where(visible, jnp.exp(masked - top), 0.0)
        probs = expo * (1.0 / jnp.sum(expo, axis=-1, keepdims=True))
        low = probs.astype(jnp.bfloat16)
        d_probs = dot(go, values, 1, 1)
        delta = jnp.sum(probs * d_probs, axis=-1, keepdims=True)
        d_scores = (probs * (d_probs - delta)).astype(jnp.bfloat16)
        out = dot(low, values, 1, 0).astype(jnp.bfloat16)
        d_query = dot(d_scores, keys, 1, 0) * scale
        for r, h in enumerate(hs):
            out_ref[:, h] = out[r * acts : (r + 1) * acts]
            dq_ref[:, h] = d_query[r * acts : (r + 1) * acts]
        d_keys = dot(d_scores, query, 0, 0) * scale
        d_values = dot(low, go, 0, 0)
        grad[0, :, cols] = d_keys[:rows].astype(jnp.bfloat16)
        grad[1, :, cols] = d_values[:rows].astype(jnp.bfloat16)
        dakv_ref[0, :, cols] = d_keys[rows:]
        dakv_ref[1, :, cols] = d_values[rows:]
    back = remote(grad.at[1 - seg], g_ref.at[seg], sems.at[3], sems.at[4], peer)
    back.start()
    local = pltpu.make_async_copy(grad.at[seg], g_ref.at[seg], sems.at[5])
    local.start()
    local.wait()
    back.wait()


def attention(heads, ratio, kvc, query, akv, grad_out, visible):
    vmem = pl.BlockSpec(memory_space=pltpu.VMEM)
    acts, width = query.shape
    return pl.pallas_call(
        functools.partial(attention_kernel, heads, ratio),
        out_shape=(
            jax.ShapeDtypeStruct((acts, width), jnp.bfloat16),
            jax.ShapeDtypeStruct((acts, width), jnp.float32),
            jax.ShapeDtypeStruct(akv.shape, jnp.float32),
            jax.ShapeDtypeStruct(kvc.shape, jnp.bfloat16),
        ),
        in_specs=[vmem] * 5,
        out_specs=(vmem,) * 4,
        scratch_shapes=[
            pltpu.VMEM(kvc.shape, jnp.bfloat16),
            pltpu.VMEM(kvc.shape, jnp.bfloat16),
            pltpu.SemaphoreType.DMA((6,)),
        ],
        compiler_params=pltpu.CompilerParams(
            collective_id=1, has_side_effects=True, vmem_limit_bytes=32 * MiB
        ),
        name="attention",
    )(kvc, query, akv, grad_out, visible)


def scatter_kernel(ndp, t_ref, o_ref, x_buf, z_send, z_buf, xs, xr, zs, zr, ys):
    nx = inner_of(ndp)
    nz = ndp // nx
    dp, seg = lax.axis_index("dp"), lax.axis_index("segment")
    z, x = dp // nx, dp % nx
    z_peer = [{"dp": ((z + o) % nz) * nx + x} for o in range(1, nz)]
    x_peer = {"dp": z * nx + (nx - 1 - x)}
    y_peer = {"segment": 1 - seg}
    greet(z_peer + ([x_peer] if nx > 1 else []) + [y_peer])
    order = sorted(range(1, nz), key=lambda o: -min(o, nz - o)) + [0]
    rows = t_ref.shape[1]
    step = min(rows, 64)
    x_copy = {}
    if nx > 1:
        for o in order:
            block = ((z + o) % nz) * nx + (nx - 1 - x)
            x_copy[o] = remote(t_ref.at[block], x_buf.at[o], xs.at[o], xr.at[o], x_peer)
            x_copy[o].start()
    z_copy = {}
    for o in order:
        block = ((z + o) % nz) * nx + x
        if nx > 1:
            x_copy[o].wait_recv()

        @pl.loop(0, rows // step)
        def _(i):
            part = pl.ds(pl.multiple_of(i * step, step), step)
            total = t_ref[block, part, :].astype(jnp.float32)
            if nx > 1:
                total = total + x_buf[o, part, :].astype(jnp.float32)
            z_send[o, part, :] = total.astype(jnp.bfloat16)

        if o > 0:
            z_copy[o] = remote(z_send.at[o], z_buf.at[o], zs.at[o], zr.at[o], z_peer[o - 1])
            z_copy[o].start()
    for copy in z_copy.values():
        copy.wait_recv()

    @pl.loop(0, rows // step)
    def _(i):
        part = pl.ds(pl.multiple_of(i * step, step), step)
        total = z_send[0, part, :].astype(jnp.float32)
        for o in range(1, nz):
            total = total + z_buf[o, part, :].astype(jnp.float32)
        z_buf[0, part, :] = total.astype(jnp.bfloat16)

    last = remote(z_buf.at[0], o_ref.at[seg], ys.at[0], ys.at[1], y_peer)
    last.start()
    local = pltpu.make_async_copy(z_buf.at[0], o_ref.at[seg], ys.at[2])
    local.start()
    local.wait()
    last.wait()
    for copy in list(x_copy.values()) + list(z_copy.values()):
        copy.wait_send()


def scatter(ndp, nseg, term):
    nx = inner_of(ndp)
    nz = ndp // nx
    dma = pltpu.SemaphoreType.DMA
    vmem = pl.BlockSpec(memory_space=pltpu.VMEM)
    block = term.shape[1:]
    return pl.pallas_call(
        functools.partial(scatter_kernel, ndp),
        out_shape=jax.ShapeDtypeStruct((nseg,) + block, jnp.bfloat16),
        in_specs=[vmem],
        out_specs=vmem,
        scratch_shapes=[pltpu.VMEM((nz,) + block, jnp.bfloat16)] * 3 + [dma((nz,))] * 4 + [dma((3,))],
        compiler_params=pltpu.CompilerParams(
            collective_id=2, has_side_effects=True, vmem_limit_bytes=40 * MiB
        ),
        name="scatter",
    )(term)


def shards(
    ndp,
    nseg,
    nmp,
    prefix_hidden,
    norm_gain,
    kv_weight,
    action_query,
    action_kv,
    out_cotangent,
    prefix_blocks,
    action_blocks,
    prefix_lengths,
    timesteps,
):
    heads_kv = kv_weight.shape[2] // HD
    ratio = QH // KVH
    columns = kv_weight.shape[2]
    seg = lax.axis_index("segment")
    wide = prefix_hidden[0].astype(jnp.float32)
    inverse = lax.rsqrt(jnp.mean(wide * wide, axis=-1, keepdims=True) + EPS)
    normed_local = (wide * inverse * norm_gain).astype(jnp.bfloat16)
    own_weight = lax.dynamic_index_in_dim(kv_weight, seg, axis=1, keepdims=False)
    weights, normed = gather(ndp, nseg, nmp, own_weight, normed_local)
    rows = nmp * normed_local.shape[0]
    width = normed_local.shape[1]
    tokens = normed.reshape(nseg * rows, width)
    projected = jnp.dot(
        tokens, weights.reshape(width, columns), preferred_element_type=jnp.float32
    )
    kvc = projected.astype(jnp.bfloat16).reshape(nseg, rows, columns)
    flow_weight = 0.5 + (timesteps[0].astype(jnp.float32) + 0.5) / STEPS
    grad_out = (flow_weight * out_cotangent[0].astype(jnp.float32)).astype(jnp.bfloat16)
    pblocks = prefix_blocks[0]
    ablocks = action_blocks[0]
    positions = jnp.arange(rows, dtype=jnp.int32)
    see_prefix = (pblocks[None, :] <= ablocks[:, None]) & (positions[None, :] < prefix_lengths[0])
    see_action = ablocks[None, :] <= ablocks[:, None]
    visible = jnp.concatenate([see_prefix, see_action], axis=1).astype(jnp.float32)
    attn_out, query_grad, d_action, grads = attention(
        heads_kv, ratio, kvc, action_query[0], action_kv[0].transpose(1, 0, 2), grad_out, visible
    )
    term = lax.dot_general(
        tokens,
        grads.reshape(nseg * rows, columns),
        (((0,), (0,)), ((), ())),
        preferred_element_type=jnp.float32,
    ).astype(jnp.bfloat16)
    summed = scatter(ndp, nseg, term.reshape(ndp, width // ndp, columns))
    weight_grad = summed.transpose(1, 0, 2).astype(jnp.float32)
    return (attn_out[None], query_grad[None], d_action.transpose(1, 0, 2)[None], weight_grad)


def solution(mesh):
    placed = (
        P(("dp", "segment"), "mp", None),
        P(),
        P("dp", None, "mp"),
        P(("dp", "segment"), None, "mp"),
        P(("dp", "segment"), None, None, "mp"),
        P(("dp", "segment"), None, "mp"),
        P(("dp", "segment"), None),
        P(("dp", "segment"), None),
        P(("dp", "segment")),
        P(("dp", "segment")),
    )
    return jax.shard_map(
        functools.partial(shards, mesh.shape["dp"], mesh.shape["segment"], mesh.shape["mp"]),
        mesh=mesh,
        in_specs=placed,
        out_specs=(
            P(("dp", "segment"), None, "mp"),
            P(("dp", "segment"), None, "mp"),
            P(("dp", "segment"), None, None, "mp"),
            P("dp", None, "mp"),
        ),
        check_vma=False,
    )
```

time: 658 us -> 333 us (0.51)
  waiting for transfers between devices: 553 us -> 0 us
  Pallas kernels: 0 us -> 283 us
  local copies, waits for them, and re-layouts: 38 us -> 17.8 us
  matrix products: 39.5 us -> 25 us
  between operations: 15.4 us -> 2.14 us
  other arithmetic: 10.5 us -> 2.98 us
    pallas_call x0 -> x3, Pallas kernels: none -> 283 us  [the longest x1 134 us: scatter(): pl.pallas_call(functools.partial(scatter_kernel, ndp), out_shape=jax.Shap...]
    reduce_scatter x1 -> x0, waiting for transfers between devices: 281 us -> none  [shards(): lax.psum_scatter(term.reshape(kv_weight.shape[0] * lax.axis_size('dp'), 2...]
    all_gather x2 -> x0, waiting for transfers between devices: 216 us -> none  [the longest x1 215 us: shards(): piece = lax.all_gather(kv_weight, 'dp', axis=0, tiled=True)]
    psum x1 -> x0, waiting for transfers between devices: 55.8 us -> none  [shards(): weight_grad = lax.psum(shard, 'segment').astype(jnp.float32)]
    unnamed x34 -> x24, local copies, waits for them, and re-layouts: 35.1 us -> 15.6 us
    dot_general x7 -> x2, matrix products: 37.4 us -> 25 us  [the longest x1 12.6 us: shards(): lax.dot_general(tokens, grads.reshape(nseg * rows, columns), (((0,), (0,)...]
  transfers between devices with their start and end apart: 4 -> 0, of which waited for: 4 -> 0; matrix products, arithmetic and copies ran while one was open for 6% -> 0% of each run, Pallas kernels for 0% -> 0%
where the time goes in v1:
time: 333 us; the launch traced here: 331 us
  Pallas kernels  283 us (85%)
  matrix products  25 us (8%)
  local copies, waits for them, and re-layouts  17.8 us (5%)
    pallas_call x1, Pallas kernels, scatter(): pl.pallas_call(functools.partial(scatter_kernel, ndp), out_shape=jax.Shap...  134 us
    pallas_call x1, Pallas kernels, gather(): pl.pallas_call(functools.partial(gather_kernel, ndp, nmp), out_shape=(jax...  120 us
    pallas_call x1, Pallas kernels, attention(): pl.pallas_call(functools.partial(attention_kernel, heads, ratio), out_sha...  28.9 us
    unnamed x24, local copies, waits for them, and re-layouts  15.6 us
    dot_general x1, matrix products, shards(): lax.dot_general(tokens, grads.reshape(nseg * rows, columns), (((0,), (0,)...  12.6 us
    dot_general x1, matrix products, shards(): jnp.dot(tokens, weights.reshape(width, columns), preferred_element_type=j...  12.5 us

profile of v1, /device:TPU:0, one launch (start us, length us, event | category | flops | bytes accessed | tf_op | source)
XLA Modules:
  0.0 330.7 jit_solution(3766064449451205115)
XLA Ops:
  0.6 0.0 copy-start
  0.6 0.0 copy-start.6
  0.7 1.6 copy-done
  2.2 0.0 copy-start.3
  2.2 2.2 constant_dynamic-slice_fusion
  4.4 0.3 copy.24
  4.7 0.0 copy-done.3
  4.7 0.9 fusion
  5.6 0.0 copy-done.6
  5.6 1.2 fusion.2.n_ref
  6.8 120.2 %gather.1 = (bf16[8,1024,512]{2,1,0:T(8,128)(2,1)S(1)}, bf16[2,2,256,8192]{3,2,1,0:T(8,128)(2,1)S(1)}) custom-call(bf16[1024,512]{1,0:T(8,128)(2,1)S(1)} %bitcast.37, bf16[256,8192]{1,0:T(8,128)(2,1)S(1)} %fusion.2.n_ref), custom_call_target="tpu_custom_call" | custom-call | tf_op jit(solution)/shard_map/gather/pallas_call | solution.py:117
  127.0 0.0 copy-start.2
  127.0 5.7 %copy-done.2 = bf16[2,2,256,8192]{3,2,1,0:T(8,128)(2,1)} copy-done((bf16[2,2,256,8192]{3,2,1,0:T(8,128)(2,1)}, bf16[2,2,256,8192]{3,2,1,0:T(8,128)(2,1)S(1)}, u32[]{:S(2)}) %copy-start.2) | copy-done | bytes 16777240
  132.8 0.0 copy-start.7
  132.8 0.0 copy-start.8
  132.8 0.0 copy-start.4
  132.8 0.0 copy-start.5
  132.8 0.0 copy-start.1
  132.8 12.5 %convolution_convert_fusion.1 = bf16[1024,512]{1,0:T(8,128)(2,1)S(1)} fusion(bf16[1024,8192]{1,0:T(8,128)(2,1)} %bitcast.44, bf16[8192,512]{1,0:T(8,128)(2,1)S(1)} %bitcast.46), kind=kOutput, calls=%fused_computation.7 | convolution fusion | flops 8590458880 | bytes 26214400 | tf_op jit(solution)/shard_map/dot_general | solution.py:323
  145.9 0.0 copy-done.7
  145.9 0.0 copy-done.8
  145.9 0.1 compare_and_fusion
  146.0 0.1 broadcast_compare_fusion
  146.8 0.0 copy-done.4
  146.9 0.0 copy-done.5
  146.9 0.0 copy-done.1
  146.9 28.9 %attention.1 = (bf16[128,1024]{1,0:T(8,128)(2,1)S(1)}, f32[128,1024]{1,0:T(8,128)S(1)}, f32[2,128,512]{2,1,0:T(8,128)S(1)}, bf16[2,512,512]{2,1,0:T(8,128)(2,1)S(1)}) custom-call(bf16[2,512,512]{2,1,0:T(8,128)(2,1)S(1)} %bitcast.39, bf16[128,1024]{1,0:T(8,128)(2,1)S(1)} %bitcast.42, bf16[2,128,512]{2,1,0:T(8,128)(2,1)S(1)} %bitcast.38, ...), custom_call_target="tpu_custom_call" | custom-call | tf_op jit(solution)/shard_map/attention/pallas_call | solution.py:199
  175.9 12.6 %convolution_convert_fusion = bf16[8192,512]{1,0:T(8,128)(2,1)S(1)} fusion(bf16[1024,8192]{1,0:T(8,128)(2,1)} %bitcast.45, bf16[1024,512]{1,0:T(8,128)(2,1)S(1)} %bitcast.47), kind=kOutput, calls=%fused_computation | convolution fusion | flops 8594128896 | bytes 26214400 | tf_op jit(solution)/shard_map/dot_general | solution.py:338
  188.4 133.8 %scatter.1 = bf16[2,1024,512]{2,1,0:T(8,128)(2,1)S(1)} custom-call(bf16[8,1024,512]{2,1,0:T(8,128)(2,1)S(1)} %bitcast.36), custom_call_target="tpu_custom_call" | custom-call | tf_op jit(solution)/shard_map/scatter/pallas_call | solution.py:283
  322.2 0.6 convert_bitcast_fusion
  322.8 5.3 %copy.20 = f32[1024,2,512]{2,1,0:T(2,128)} copy(f32[1024,2,512]{2,0,1:T(8,128)S(1)} %convert_bitcast_fusion) | data formatting | bytes 8388608
  328.0 1.2 copy.19
  329.2 0.7 copy.30
  329.9 0.8 copy.31
  (5 shorter events, 0.1 us)
Async XLA Ops:
  0.6 1.6 copy-start
  0.6 5.0 %copy-start.6 = (f32[8192]{0:T(1024)S(1)}, f32[8192]{0:T(1024)}, u32[]{:S(2)}) copy-start(f32[8192]{0:T(1024)} %param.11) | copy-start | bytes 98308
  2.2 2.5 copy-start.3
  127.0 5.7 %copy-start.2 = (bf16[2,2,256,8192]{3,2,1,0:T(8,128)(2,1)}, bf16[2,2,256,8192]{3,2,1,0:T(8,128)(2,1)S(1)}, u32[]{:S(2)}) copy-start(bf16[2,2,256,8192]{3,2,1,0:T(8,128)(2,1)S(1)} %get-tuple-element.10) | copy-start | bytes 50331652
  132.8 13.1 %copy-start.7 = (s32[1,128]{1,0:T(1,128)S(1)}, s32[1,128]{1,0:T(1,128)}, u32[]{:S(2)}) copy-start(s32[1,128]{1,0:T(1,128)} %param.17) | copy-start | bytes 1540
  132.8 13.2 %copy-start.8 = (s32[1,512]{1,0:T(1,128)S(1)}, s32[1,512]{1,0:T(1,128)}, u32[]{:S(2)}) copy-start(s32[1,512]{1,0:T(1,128)} %param.16) | copy-start | bytes 6148
  132.8 14.1 %copy-start.4 = (bf16[1,128,1024]{2,1,0:T(8,128)(2,1)S(1)}, bf16[1,128,1024]{2,1,0:T(8,128)(2,1)}, u32[]{:S(2)}) copy-start(bf16[1,128,1024]{2,1,0:T(8,128)(2,1)} %param.15) | copy-start | bytes 786436
  132.8 14.1 %copy-start.5 = (bf16[1,128,2,512]{3,2,1,0:T(2,128)(2,1)S(1)}, bf16[1,128,2,512]{3,2,1,0:T(2,128)(2,1)}, u32[]{:S(2)}) copy-start(bf16[1,128,2,512]{3,2,1,0:T(2,128)(2,1)} %param.14) | copy-start | bytes 786436
  132.8 14.2 %copy-start.1 = (bf16[1,128,1024]{2,1,0:T(8,128)(2,1)S(1)}, bf16[1,128,1024]{2,1,0:T(8,128)(2,1)}, u32[]{:S(2)}) copy-start(bf16[1,128,1024]{2,1,0:T(8,128)(2,1)} %param.13) | copy-start | bytes 786436

commit v2 on v1

--- a/solution.py
+++ b/solution.py
@@ -43,8 +43,8 @@
     pl.semaphore_wait(barrier, len(peers))
 
 
-def gather_kernel(
-    ndp, nmp, w_ref, n_ref, w_all, n_all,
+def project_kernel(
+    ndp, nmp, w_ref, n_ref, kvc_ref, n_all, w_all, acc,
     own_sem, zs, zr, xs, xr, ys, yr, ms, mr, fs, fr,
 ):
     nx = inner_of(ndp)
@@ -56,84 +56,131 @@
     y_peer = {"segment": 1 - seg}
     m_peer = [{"mp": (mp + o) % nmp} for o in range(1, nmp)]
     greet(z_peer + ([x_peer] if nx > 1 else []) + [y_peer] + m_peer)
-    rows = n_ref.shape[0] // CHUNKS
+    depth = w_ref.shape[0]
+    step = depth // CHUNKS
+    mine, theirs = seg * nmp + mp, (1 - seg) * nmp + mp
+    order = [0] + sorted(range(1, nz), key=lambda o: min(o, nz - o))
+
+    def outer(o):
+        return (z + nz - o) % nz
+
+    def columns(o):
+        return pl.ds(pl.multiple_of(outer(o) * (nx * depth), nx * depth), nx * depth)
+
+    def z_copy(o, c):
+        part = pl.ds(c * step, step)
+        return remote(w_ref.at[part], w_all.at[dp, part], zs.at[o - 1, c], zr.at[o - 1, c], z_peer[o - 1])
+
+    def x_copy(o, c):
+        part = pl.ds(c * step, step)
+        src = outer(o) * nx + x
+        held = w_ref.at[part] if o == 0 else w_all.at[src, part]
+        return remote(held, w_all.at[src, part], xs.at[o, c], xr.at[o, c], x_peer)
+
+    def y_copy(o):
+        return remote(n_ref.at[:, columns(o)], n_all.at[mine, :, columns(o)], ys.at[o], yr.at[o], y_peer)
+
+    def m_copy(p):
+        return remote(n_ref, n_all.at[mine], ms.at[p], mr.at[p], m_peer[p])
+
+    def f_copy(o, p):
+        part = n_all.at[theirs, :, columns(o)]
+        return remote(part, part, fs.at[o, p], fr.at[o, p], m_peer[p])
 
     own_w = pltpu.make_async_copy(w_ref, w_all.at[dp], own_sem.at[0])
-    own_n = pltpu.make_async_copy(n_ref, n_all.at[seg, mp], own_sem.at[1])
-    started = []
-    order = sorted(range(1, nz), key=lambda o: min(o, nz - o))
-    z_copy = {o: remote(w_ref, w_all.at[dp], zs.at[o - 1], zr.at[o - 1], z_peer[o - 1]) for o in order}
-    y_copy = [
-        remote(
-            n_ref.at[pl.ds(c * rows, rows)],
-            n_all.at[seg, mp, pl.ds(c * rows, rows)],
-            ys.at[c], yr.at[c], y_peer,
-        )
-        for c in range(CHUNKS)
-    ]
-    x_copy = []
+    own_n = pltpu.make_async_copy(n_ref, n_all.at[mine], own_sem.at[1])
+    for o in order[1:]:
+        for c in range(CHUNKS):
+            z_copy(o, c).start()
     if nx > 1:
-        x_copy.append(remote(w_ref, w_all.at[dp], xs.at[0], xr.at[0], x_peer))
-    m_copy = [remote(n_ref, n_all.at[seg, mp], ms.at[o], mr.at[o], m_peer[o]) for o in range(nmp - 1)]
-    for copy in list(z_copy.values()) + x_copy + y_copy + m_copy + [own_w, own_n]:
-        copy.start()
-    f_copy = []
-
-    def on_z(o):
-        z_copy[o].wait_recv()
+        for c in range(CHUNKS):
+            x_copy(0, c).start()
+    for o in order:
+        y_copy(o).start()
+    for p in range(nmp - 1):
+        m_copy(p).start()
+    own_w.start()
+    own_n.start()
+    acc[...] = jnp.zeros_like(acc)
+
+    def multiply(block):
+        cols = pl.ds(pl.multiple_of(block * depth, depth), depth)
+
+        @pl.loop(0, n_all.shape[0])
+        def _(i):
+            acc[i] += jnp.dot(n_all[i, :, cols], w_all[block], preferred_element_type=jnp.float32)
+
+    def finish(o):
+        for p in range(nmp - 1):
+            f_copy(o, p).wait_recv()
+        if o == 0:
+            own_w.wait()
+            own_n.wait()
+            for p in range(nmp - 1):
+                m_copy(p).wait_recv()
+        multiply(outer(o) * nx + x)
         if nx > 1:
-            src = ((z + nz - o) % nz) * nx + x
-            copy = remote(w_all.at[src], w_all.at[src], xs.at[o], xr.at[o], x_peer)
-            copy.start()
-            x_copy.append(copy)
-
-    def on_y(c):
-        y_copy[c].wait_recv()
-        for o in range(nmp - 1):
-            part = n_all.at[1 - seg, mp, pl.ds(c * rows, rows)]
-            copy = remote(part, part, fs.at[o, c], fr.at[o, c], m_peer[o])
-            copy.start()
-            f_copy.append(copy)
-
-    for i in range(max(len(order), CHUNKS)):
-        if i < len(order):
-            on_z(order[i])
-        if i < CHUNKS:
-            on_y(i)
-    own_w.wait()
-    own_n.wait()
-    for copy in m_copy + x_copy + f_copy:
-        copy.wait_recv()
-    for copy in list(z_copy.values()) + y_copy + m_copy + x_copy + f_copy:
-        copy.wait_send()
-
-
-def gather(ndp, nseg, nmp, weight, normed):
+            for c in range(CHUNKS):
+                x_copy(o, c).wait_recv()
+            multiply(outer(o) * nx + (nx - 1 - x))
+
+    for i, o in enumerate(order):
+        if o > 0:
+            for c in range(CHUNKS):
+                z_copy(o, c).wait_recv()
+                if nx > 1:
+                    x_copy(o, c).start()
+        y_copy(o).wait_recv()
+        for p in range(nmp - 1):
+            f_copy(o, p).start()
+        if i > 0:
+            finish(order[i - 1])
+    finish(order[-1])
+    kvc_ref[...] = acc[...].astype(kvc_ref.dtype)
+    for o in order:
+        if o > 0:
+            for c in range(CHUNKS):
+                z_copy(o, c).wait_send()
+        if nx > 1:
+            for c in range(CHUNKS):
+                x_copy(o, c).wait_send()
+        y_copy(o).wait_send()
+        for p in range(nmp - 1):
+            f_copy(o, p).wait_send()
+    for p in range(nmp - 1):
+        m_copy(p).wait_send()
+
+
+def project(ndp, nseg, nmp, weight, normed):
     nx = inner_of(ndp)
     nz = ndp // nx
     dma = pltpu.SemaphoreType.DMA
     vmem = pl.BlockSpec(memory_space=pltpu.VMEM)
-    anys = pl.BlockSpec(memory_space=pl.ANY)
+    rows, width = normed.shape
+    cols = weight.shape[1]
+    others, further = max(nmp - 1, 1), max(nz - 1, 1)
     return pl.pallas_call(
-        functools.partial(gather_kernel, ndp, nmp),
+        functools.partial(project_kernel, ndp, nmp),
         out_shape=(
-            jax.ShapeDtypeStruct((ndp,) + weight.shape, weight.dtype),
-            jax.ShapeDtypeStruct((nseg, nmp) + normed.shape, normed.dtype),
+            jax.ShapeDtypeStruct((nseg * nmp, rows, cols), jnp.bfloat16),
+            jax.ShapeDtypeStruct((nseg * nmp, rows, width), normed.dtype),
         ),
         in_specs=[vmem, vmem],
-        out_specs=(anys, anys),
+        out_specs=(vmem, vmem),
         scratch_shapes=[
+            pltpu.VMEM((ndp,) + weight.shape, weight.dtype),
+            pltpu.VMEM((nseg * nmp, rows, cols), jnp.float32),
             dma((2,)),
-            dma((max(nz - 1, 1),)), dma((max(nz - 1, 1),)),
+            dma((further, CHUNKS)), dma((further, CHUNKS)),
+            dma((nz, CHUNKS)), dma((nz, CHUNKS)),
             dma((nz,)), dma((nz,)),
-            dma((CHUNKS,)), dma((CHUNKS,)),
-            dma((max(nmp - 1, 1),)), dma((max(nmp - 1, 1),)),
-            dma((max(nmp - 1, 1), CHUNKS)), dma((max(nmp - 1, 1), CHUNKS)),
+            dma((others,)), dma((others,)),
+            dma((nz, others)), dma((nz, others)),
         ],
         compiler_params=pltpu.CompilerParams(
-            collective_id=0, has_side_effects=True, vmem_limit_bytes=16 * MiB
-        ),
-        name="gather",
+            collective_id=0, has_side_effects=True, vmem_limit_bytes=20 * MiB
+        ),
+        name="project",
     )(weight, normed)
 
 
@@ -212,13 +259,13 @@
             pltpu.SemaphoreType.DMA((6,)),
         ],
         compiler_params=pltpu.CompilerParams(
-            collective_id=1, has_side_effects=True, vmem_limit_bytes=32 * MiB
+            collective_id=1, has_side_effects=True, vmem_limit_bytes=12 * MiB
         ),
         name="attention",
     )(kvc, query, akv, grad_out, visible)
 
 
-def scatter_kernel(ndp, t_ref, o_ref, x_buf, z_send, z_buf, xs, xr, zs, zr, ys):
+def scatter_kernel(ndp, n_ref, g_ref, o_ref, x_send, x_buf, z_send, z_buf, xs, xr, zs, zr, ys, yr):
     nx = inner_of(ndp)
     nz = ndp // nx
     dp, seg = lax.axis_index("dp"), lax.axis_index("segment")
@@ -228,69 +275,81 @@
     y_peer = {"segment": 1 - seg}
     greet(z_peer + ([x_peer] if nx > 1 else []) + [y_peer])
     order = sorted(range(1, nz), key=lambda o: -min(o, nz - o)) + [0]
-    rows = t_ref.shape[1]
-    step = min(rows, 64)
-    x_copy = {}
+    rows = o_ref.shape[1]
+    step = min(rows, max(rows // CHUNKS, 128))
+    steps = rows // step
+
+    def part(c):
+        return pl.ds(pl.multiple_of(c * step, step), step)
+
+    def term(block, c):
+        cols = pl.ds(pl.multiple_of(block * rows + c * step, step), step)
+        return lax.dot_general(
+            n_ref[:, cols], g_ref[...], (((0,), (0,)), ((), ())), preferred_element_type=jnp.float32
+        )
+
+    def x_copy(o, c):
+        return remote(x_send.at[o, part(c)], x_buf.at[o, part(c)], xs.at[o, c], xr.at[o, c], x_peer)
+
+    def z_copy(o, c):
+        return remote(z_send.at[o, part(c)], z_buf.at[o, part(c)], zs.at[o, c], zr.at[o, c], z_peer[o - 1])
+
+    def y_copy(c):
+        return remote(o_ref.at[seg, part(c)], o_ref.at[seg, part(c)], ys.at[c], yr.at[c], y_peer)
+
     if nx > 1:
         for o in order:
-            block = ((z + o) % nz) * nx + (nx - 1 - x)
-            x_copy[o] = remote(t_ref.at[block], x_buf.at[o], xs.at[o], xr.at[o], x_peer)
-            x_copy[o].start()
-    z_copy = {}
+            @pl.loop(0, steps)
+            def _(c):
+                x_send[o, part(c), :] = term(((z + o) % nz) * nx + (nx - 1 - x), c).astype(jnp.bfloat16)
+                x_copy(o, c).start()
+
     for o in order:
-        block = ((z + o) % nz) * nx + x
-        if nx > 1:
-            x_copy[o].wait_recv()
-
-        @pl.loop(0, rows // step)
-        def _(i):
-            part = pl.ds(pl.multiple_of(i * step, step), step)
-            total = t_ref[block, part, :].astype(jnp.float32)
+        @pl.loop(0, steps)
+        def _(c):
+            total = term(((z + o) % nz) * nx + x, c)
             if nx > 1:
-                total = total + x_buf[o, part, :].astype(jnp.float32)
-            z_send[o, part, :] = total.astype(jnp.bfloat16)
-
-        if o > 0:
-            z_copy[o] = remote(z_send.at[o], z_buf.at[o], zs.at[o], zr.at[o], z_peer[o - 1])
-            z_copy[o].start()
-    for copy in z_copy.values():
-        copy.wait_recv()
-
-    @pl.loop(0, rows // step)
-    def _(i):
-        part = pl.ds(pl.multiple_of(i * step, step), step)
-        total = z_send[0, part, :].astype(jnp.float32)
-        for o in range(1, nz):
-            total = total + z_buf[o, part, :].astype(jnp.float32)
-        z_buf[0, part, :] = total.astype(jnp.bfloat16)
-
-    last = remote(z_buf.at[0], o_ref.at[seg], ys.at[0], ys.at[1], y_peer)
-    last.start()
-    local = pltpu.make_async_copy(z_buf.at[0], o_ref.at[seg], ys.at[2])
-    local.start()
-    local.wait()
-    last.wait()
-    for copy in list(x_copy.values()) + list(z_copy.values()):
-        copy.wait_send()
-
-
-def scatter(ndp, nseg, term):
+                x_copy(o, c).wait_recv()
+                total = total + x_buf[o, part(c), :].astype(jnp.float32)
+            if o > 0:
+                z_send[o, part(c), :] = total.astype(jnp.bfloat16)
+                z_copy(o, c).start()
+            else:
+                for other in order[:-1]:
+                    z_copy(other, c).wait_recv()
+                    total = total + z_buf[other, part(c), :].astype(jnp.float32)
+                o_ref[seg, part(c), :] = total.astype(jnp.bfloat16)
+                y_copy(c).start()
+
+    @pl.loop(0, steps)
+    def _(c):
+        y_copy(c).wait()
+        for o in order:
+            if nx > 1:
+                x_copy(o, c).wait_send()
+            if o > 0:
+                z_copy(o, c).wait_send()
+
+
+def scatter(ndp, nseg, tokens, grads):
     nx = inner_of(ndp)
     nz = ndp // nx
     dma = pltpu.SemaphoreType.DMA
     vmem = pl.BlockSpec(memory_space=pltpu.VMEM)
-    block = term.shape[1:]
+    block = (tokens.shape[1] // ndp, grads.shape[1])
     return pl.pallas_call(
         functools.partial(scatter_kernel, ndp),
         out_shape=jax.ShapeDtypeStruct((nseg,) + block, jnp.bfloat16),
-        in_specs=[vmem],
+        in_specs=[vmem, vmem],
         out_specs=vmem,
-        scratch_shapes=[pltpu.VMEM((nz,) + block, jnp.bfloat16)] * 3 + [dma((nz,))] * 4 + [dma((3,))],
+        scratch_shapes=[pltpu.VMEM((nz,) + block, jnp.bfloat16)] * 4
+        + [dma((nz, CHUNKS))] * 4
+        + [dma((CHUNKS,))] * 2,
         compiler_params=pltpu.CompilerParams(
-            collective_id=2, has_side_effects=True, vmem_limit_bytes=40 * MiB
+            collective_id=2, has_side_effects=True, vmem_limit_bytes=24 * MiB
         ),
         name="scatter",
-    )(term)
+    )(tokens, grads)
 
 
 def shards(
@@ -316,14 +375,10 @@
     inverse = lax.rsqrt(jnp.mean(wide * wide, axis=-1, keepdims=True) + EPS)
     normed_local = (wide * inverse * norm_gain).astype(jnp.bfloat16)
     own_weight = lax.dynamic_index_in_dim(kv_weight, seg, axis=1, keepdims=False)
-    weights, normed = gather(ndp, nseg, nmp, own_weight, normed_local)
+    kvc, tokens = project(ndp, nseg, nmp, own_weight, normed_local)
     rows = nmp * normed_local.shape[0]
     width = normed_local.shape[1]
-    tokens = normed.reshape(nseg * rows, width)
-    projected = jnp.dot(
-        tokens, weights.reshape(width, columns), preferred_element_type=jnp.float32
-    )
-    kvc = projected.astype(jnp.bfloat16).reshape(nseg, rows, columns)
+    kvc = kvc.reshape(nseg, rows, columns)
     flow_weight = 0.5 + (timesteps[0].astype(jnp.float32) + 0.5) / STEPS
     grad_out = (flow_weight * out_cotangent[0].astype(jnp.float32)).astype(jnp.bfloat16)
     pblocks = prefix_blocks[0]
@@ -335,13 +390,9 @@
     attn_out, query_grad, d_action, grads = attention(
         heads_kv, ratio, kvc, action_query[0], action_kv[0].transpose(1, 0, 2), grad_out, visible
     )
-    term = lax.dot_general(
-        tokens,
-        grads.reshape(nseg * rows, columns),
-        (((0,), (0,)), ((), ())),
-        preferred_element_type=jnp.float32,
-    ).astype(jnp.bfloat16)
-    summed = scatter(ndp, nseg, term.reshape(ndp, width // ndp, columns))
+    summed = scatter(
+        ndp, nseg, tokens.reshape(nseg * rows, width), grads.reshape(nseg * rows, columns)
+    )
     weight_grad = summed.transpose(1, 0, 2).astype(jnp.float32)
     return (attn_out[None], query_grad[None], d_action.transpose(1, 0, 2)[None], weight_grad)
 

time: 333 us -> 258 us (0.77)
  Pallas kernels: 283 us -> 241 us
  matrix products: 25 us -> 0 us
  local copies, waits for them, and re-layouts: 17.8 us -> 12 us
    pallas_call x1, Pallas kernels: 134 us -> 106 us  [scatter(): pl.pallas_call(functools.partial(scatter_kernel, ndp), out_shape=jax.Shap...]
    dot_general x2 -> x0, matrix products: 25 us -> none  [the longest x1 12.6 us: shards(): lax.dot_general(tokens, grads.reshape(nseg * rows, columns), (((0,), (0,)...]
    pallas_call x1, Pallas kernels: 120 us -> 106 us  [project(): pl.pallas_call(functools.partial(project_kernel, ndp, nmp), out_shape=(ja...]
    unnamed x24 -> x22, local copies, waits for them, and re-layouts: 15.6 us -> 9.89 us
where the time goes in v2:
time: 258 us
  Pallas kernels  241 us (93%)
  local copies, waits for them, and re-layouts  12 us (5%)
  other arithmetic  2.98 us (1%)
    pallas_call x1, Pallas kernels, scatter(): pl.pallas_call(functools.partial(scatter_kernel, ndp), out_shape=jax.Shap...  106 us
    pallas_call x1, Pallas kernels, project(): pl.pallas_call(functools.partial(project_kernel, ndp, nmp), out_shape=(ja...  106 us
    pallas_call x1, Pallas kernels, attention(): pl.pallas_call(functools.partial(attention_kernel, heads, ratio), out_sha...  28.9 us
    unnamed x22, local copies, waits for them, and re-layouts  9.89 us

profile of v2, /device:TPU:0, one launch (start us, length us, event | category | flops | bytes accessed | tf_op | source)
XLA Modules:
  0.0 257.9 jit_solution(8673086053616229514)
XLA Ops:
  0.6 0.0 copy-start
  0.6 1.6 copy-done
  2.2 0.0 copy-start.2
  2.2 2.2 constant_dynamic-slice_fusion
  4.4 0.0 copy-start.5
  4.4 0.3 copy.24
  4.7 0.0 copy-done.2
  4.7 0.9 fusion
  5.6 0.0 copy-done.5
  5.6 1.2 fusion.2.n_ref
  6.8 0.0 copy-start.6
  6.9 0.0 copy-start.7
  6.9 0.0 copy-start.3
  6.9 0.0 copy-start.4
  6.9 0.0 copy-start.1
  6.9 105.6 %project.1 = (bf16[4,256,512]{2,1,0:T(8,128)(2,1)S(1)}, bf16[4,256,8192]{2,1,0:T(8,128)(2,1)S(1)}) custom-call(bf16[1024,512]{1,0:T(8,128)(2,1)S(1)} %bitcast.31, bf16[256,8192]{1,0:T(8,128)(2,1)S(1)} %fusion.2.n_ref), custom_call_target="tpu_custom_call" | custom-call | tf_op jit(solution)/shard_map/project/pallas_call | solution.py:162
  113.2 0.0 copy-done.6
  113.2 0.0 copy-done.7
  113.2 0.1 compare_and_fusion
  113.3 0.1 broadcast_compare_fusion
  114.1 0.0 copy-done.3
  114.1 0.0 copy-done.4
  114.2 0.0 copy-done.1
  114.2 28.9 %attention.1 = (bf16[128,1024]{1,0:T(8,128)(2,1)S(1)}, f32[128,1024]{1,0:T(8,128)S(1)}, f32[2,128,512]{2,1,0:T(8,128)S(1)}, bf16[2,512,512]{2,1,0:T(8,128)(2,1)S(1)}) custom-call(bf16[2,512,512]{2,1,0:T(8,128)(2,1)S(1)} %bitcast.34, bf16[128,1024]{1,0:T(8,128)(2,1)S(1)} %bitcast.37, bf16[2,128,512]{2,1,0:T(8,128)(2,1)S(1)} %bitcast.33, ...), custom_call_target="tpu_custom_call" | custom-call | tf_op jit(solution)/shard_map/attention/pallas_call | solution.py:246
  143.1 106.3 %scatter.1 = bf16[2,1024,512]{2,1,0:T(8,128)(2,1)S(1)} custom-call(bf16[1024,8192]{1,0:T(8,128)(2,1)S(1)} %bitcast.30, bf16[1024,512]{1,0:T(8,128)(2,1)S(1)} %bitcast.32), custom_call_target="tpu_custom_call" | custom-call | tf_op jit(solution)/shard_map/scatter/pallas_call | solution.py:340
  249.4 0.6 convert_bitcast_fusion
  250.0 5.3 %copy.20 = f32[1024,2,512]{2,1,0:T(2,128)} copy(f32[1024,2,512]{2,0,1:T(8,128)S(1)} %convert_bitcast_fusion) | data formatting | bytes 8388608
  255.3 1.2 copy.19
  256.4 0.7 copy.30
  257.2 0.8 copy.31
  (5 shorter events, 0.1 us)
Async XLA Ops:
  0.6 1.6 copy-start
  2.2 2.5 copy-start.2
  4.4 1.2 copy-start.5
  6.8 106.3 %copy-start.6 = (s32[1,128]{1,0:T(1,128)S(1)}, s32[1,128]{1,0:T(1,128)}, u32[]{:S(2)}) copy-start(s32[1,128]{1,0:T(1,128)} %param.17) | copy-start | bytes 1540
  6.9 106.3 %copy-start.7 = (s32[1,512]{1,0:T(1,128)S(1)}, s32[1,512]{1,0:T(1,128)}, u32[]{:S(2)}) copy-start(s32[1,512]{1,0:T(1,128)} %param.16) | copy-start | bytes 6148
  6.9 107.2 %copy-start.3 = (bf16[1,128,1024]{2,1,0:T(8,128)(2,1)S(1)}, bf16[1,128,1024]{2,1,0:T(8,128)(2,1)}, u32[]{:S(2)}) copy-start(bf16[1,128,1024]{2,1,0:T(8,128)(2,1)} %param.15) | copy-start | bytes 786436
  6.9 107.3 %copy-start.4 = (bf16[1,128,2,512]{3,2,1,0:T(2,128)(2,1)S(1)}, bf16[1,128,2,512]{3,2,1,0:T(2,128)(2,1)}, u32[]{:S(2)}) copy-start(bf16[1,128,2,512]{3,2,1,0:T(2,128)(2,1)} %param.14) | copy-start | bytes 786436
  6.9 107.3 %copy-start.1 = (bf16[1,128,1024]{2,1,0:T(8,128)(2,1)S(1)}, bf16[1,128,1024]{2,1,0:T(8,128)(2,1)}, u32[]{:S(2)}) copy-start(bf16[1,128,1024]{2,1,0:T(8,128)(2,1)} %param.13) | copy-start | bytes 786436

commit v3 on v2

--- a/solution.py
+++ b/solution.py
@@ -51,56 +51,78 @@
     nz = ndp // nx
     dp, seg, mp = lax.axis_index("dp"), lax.axis_index("segment"), lax.axis_index("mp")
     z, x = dp // nx, dp % nx
-    z_peer = [{"dp": ((z + o) % nz) * nx + x} for o in range(1, nz)]
+    up, down = {"dp": ((z + 1) % nz) * nx + x}, {"dp": ((z + nz - 1) % nz) * nx + x}
     x_peer = {"dp": z * nx + (nx - 1 - x)}
     y_peer = {"segment": 1 - seg}
     m_peer = [{"mp": (mp + o) % nmp} for o in range(1, nmp)]
-    greet(z_peer + ([x_peer] if nx > 1 else []) + [y_peer] + m_peer)
+    near = [up, down] if nz > 2 else [up] if nz > 1 else []
+    greet(near + ([x_peer] if nx > 1 else []) + [y_peer] + m_peer)
     depth = w_ref.shape[0]
     step = depth // CHUNKS
     mine, theirs = seg * nmp + mp, (1 - seg) * nmp + mp
-    order = [0] + sorted(range(1, nz), key=lambda o: min(o, nz - o))
-
-    def outer(o):
-        return (z + nz - o) % nz
-
-    def columns(o):
-        return pl.ds(pl.multiple_of(outer(o) * (nx * depth), nx * depth), nx * depth)
-
-    def z_copy(o, c):
-        part = pl.ds(c * step, step)
-        return remote(w_ref.at[part], w_all.at[dp, part], zs.at[o - 1, c], zr.at[o - 1, c], z_peer[o - 1])
-
-    def x_copy(o, c):
-        part = pl.ds(c * step, step)
-        src = outer(o) * nx + x
-        held = w_ref.at[part] if o == 0 else w_all.at[src, part]
-        return remote(held, w_all.at[src, part], xs.at[o, c], xr.at[o, c], x_peer)
-
-    def y_copy(o):
-        return remote(n_ref.at[:, columns(o)], n_all.at[mine, :, columns(o)], ys.at[o], yr.at[o], y_peer)
+
+    def columns(src):
+        return pl.ds(pl.multiple_of(src * (nx * depth), nx * depth), nx * depth)
+
+    def part(c):
+        return pl.ds(pl.multiple_of(c * step, step), step)
+
+    def hop(src, c, rising):
+        held = w_all.at[src * nx + x, part(c)]
+        side = 0 if rising else 1
+        return remote(held, held, zs.at[side, src, c], zr.at[src, c], up if rising else down)
+
+    def x_copy(src, c):
+        held = w_all.at[src * nx + x, part(c)]
+        return remote(held, held, xs.at[src, c], xr.at[src, c], x_peer)
+
+    def y_copy(src):
+        return remote(n_ref.at[:, columns(src)], n_all.at[mine, :, columns(src)], ys.at[src], yr.at[src], y_peer)
 
     def m_copy(p):
         return remote(n_ref, n_all.at[mine], ms.at[p], mr.at[p], m_peer[p])
 
-    def f_copy(o, p):
-        part = n_all.at[theirs, :, columns(o)]
-        return remote(part, part, fs.at[o, p], fr.at[o, p], m_peer[p])
+    def f_copy(src, p):
+        held = n_all.at[theirs, :, columns(src)]
+        return remote(held, held, fs.at[src, p], fr.at[src, p], m_peer[p])
+
+    def at_level(level, act):
+        @pl.when(z - level >= 0)
+        def _():
+            act(z - level, True)
+
+        @pl.when(z + level < nz)
+        def _():
+            act(z + level, False)
+
+    def send_on(src, c, rising):
+        if rising:
+            @pl.when(z < nz - 1)
+            def _():
+                hop(src, c, True).start()
+        else:
+            @pl.when(z > 0)
+            def _():
+                hop(src, c, False).start()
 
     own_w = pltpu.make_async_copy(w_ref, w_all.at[dp], own_sem.at[0])
     own_n = pltpu.make_async_copy(n_ref, n_all.at[mine], own_sem.at[1])
-    for o in order[1:]:
-        for c in range(CHUNKS):
-            z_copy(o, c).start()
-    if nx > 1:
-        for c in range(CHUNKS):
-            x_copy(0, c).start()
-    for o in order:
-        y_copy(o).start()
+    own_w.start()
+    own_n.start()
+    y_copy(z).start()
     for p in range(nmp - 1):
         m_copy(p).start()
-    own_w.start()
-    own_n.start()
+    own_w.wait()
+    for c in range(CHUNKS):
+        send_on(z, c, True)
+        send_on(z, c, False)
+        if nx > 1:
+            x_copy(z, c).start()
+
+    @pl.loop(1, nz)
+    def _(level):
+        at_level(level, lambda src, rising: y_copy(src).start())
+
     acc[...] = jnp.zeros_like(acc)
 
     def multiply(block):
@@ -110,43 +132,71 @@
         def _(i):
             acc[i] += jnp.dot(n_all[i, :, cols], w_all[block], preferred_element_type=jnp.float32)
 
-    def finish(o):
+    def relay(level):
+        @pl.loop(0, CHUNKS)
+        def _(c):
+            def pass_on(src, rising):
+                hop(src, c, rising).wait_recv()
+                send_on(src, c, rising)
+                if nx > 1:
+                    x_copy(src, c).start()
+
+            at_level(level, pass_on)
+
+    def share(src):
+        y_copy(src).wait_recv()
         for p in range(nmp - 1):
-            f_copy(o, p).wait_recv()
-        if o == 0:
-            own_w.wait()
-            own_n.wait()
-            for p in range(nmp - 1):
-                m_copy(p).wait_recv()
-        multiply(outer(o) * nx + x)
+            f_copy(src, p).start()
+
+    def finish(src):
+        for p in range(nmp - 1):
+            f_copy(src, p).wait_recv()
+        multiply(src * nx + x)
         if nx > 1:
-            for c in range(CHUNKS):
-                x_copy(o, c).wait_recv()
-            multiply(outer(o) * nx + (nx - 1 - x))
-
-    for i, o in enumerate(order):
-        if o > 0:
-            for c in range(CHUNKS):
-                z_copy(o, c).wait_recv()
-                if nx > 1:
-                    x_copy(o, c).start()
-        y_copy(o).wait_recv()
+            @pl.loop(0, CHUNKS)
+            def _(c):
+                x_copy(src, c).wait_recv()
+
+            multiply(src * nx + (nx - 1 - x))
+
+    share(z)
+    if nz > 1:
+        relay(1)
+        at_level(1, lambda src, rising: share(src))
+    own_n.wait()
+    for p in range(nmp - 1):
+        m_copy(p).wait_recv()
+    finish(z)
+
+    @pl.loop(2, nz)
+    def _(level):
+        relay(level)
+        at_level(level, lambda src, rising: share(src))
+        at_level(level - 1, lambda src, rising: finish(src))
+
+    if nz > 1:
+        at_level(nz - 1, lambda src, rising: finish(src))
+    kvc_ref[...] = acc[...].astype(kvc_ref.dtype)
+
+    @pl.loop(0, nz)
+    def _(src):
+        @pl.loop(0, CHUNKS)
+        def _(c):
+            @pl.when((src <= z) & (z < nz - 1))
+            def _():
+                hop(src, c, True).wait_send()
+
+            @pl.when((src >= z) & (z > 0))
+            def _():
+                hop(src, c, False).wait_send()
+
+            if nx > 1:
+                x_copy(src, c).wait_send()
+
+        y_copy(src).wait_send()
         for p in range(nmp - 1):
-            f_copy(o, p).start()
-        if i > 0:
-            finish(order[i - 1])
-    finish(order[-1])
-    kvc_ref[...] = acc[...].astype(kvc_ref.dtype)
-    for o in order:
-        if o > 0:
-            for c in range(CHUNKS):
-                z_copy(o, c).wait_send()
-        if nx > 1:
-            for c in range(CHUNKS):
-                x_copy(o, c).wait_send()
-        y_copy(o).wait_send()
-        for p in range(nmp - 1):
-            f_copy(o, p).wait_send()
+            f_copy(src, p).wait_send()
+
     for p in range(nmp - 1):
         m_copy(p).wait_send()
 
@@ -158,7 +208,7 @@
     vmem = pl.BlockSpec(memory_space=pltpu.VMEM)
     rows, width = normed.shape
     cols = weight.shape[1]
-    others, further = max(nmp - 1, 1), max(nz - 1, 1)
+    others = max(nmp - 1, 1)
     return pl.pallas_call(
         functools.partial(project_kernel, ndp, nmp),
         out_shape=(
@@ -171,7 +221,7 @@
             pltpu.VMEM((ndp,) + weight.shape, weight.dtype),
             pltpu.VMEM((nseg * nmp, rows, cols), jnp.float32),
             dma((2,)),
-            dma((further, CHUNKS)), dma((further, CHUNKS)),
+            dma((2, nz, CHUNKS)), dma((nz, CHUNKS)),
             dma((nz, CHUNKS)), dma((nz, CHUNKS)),
             dma((nz,)), dma((nz,)),
             dma((others,)), dma((others,)),

time: 258 us -> 261 us (1.012)
  Pallas kernels: 241 us -> 244 us
    pallas_call x1, Pallas kernels: 28.9 us -> 22.7 us  [attention(): pl.pallas_call(functools.partial(attention_kernel, heads, ratio), out_sha...]
    pallas_call x1, Pallas kernels: 106 us -> 111 us  [project(): pl.pallas_call(functools.partial(project_kernel, ndp, nmp), out_shape=(ja...]
    pallas_call x1, Pallas kernels: 106 us -> 110 us  [scatter(): pl.pallas_call(functools.partial(scatter_kernel, ndp), out_shape=jax.Shap...]
where the time goes in v3:
time: 261 us
  Pallas kernels  244 us (93%)
  local copies, waits for them, and re-layouts  12 us (5%)
  other arithmetic  2.98 us (1%)
    pallas_call x1, Pallas kernels, project(): pl.pallas_call(functools.partial(project_kernel, ndp, nmp), out_shape=(ja...  111 us
    pallas_call x1, Pallas kernels, scatter(): pl.pallas_call(functools.partial(scatter_kernel, ndp), out_shape=jax.Shap...  110 us
    pallas_call x1, Pallas kernels, attention(): pl.pallas_call(functools.partial(attention_kernel, heads, ratio), out_sha...  22.7 us
    unnamed x22, local copies, waits for them, and re-layouts  9.89 us

profile of v3, /device:TPU:0, one launch (start us, length us, event | category | flops | bytes accessed | tf_op | source)
XLA Modules:
  0.0 261.1 jit_solution(12877993156075104570)
XLA Ops:
  0.6 0.0 copy-start
  0.6 1.6 copy-done
  2.2 0.0 copy-start.2
  2.2 2.2 constant_dynamic-slice_fusion
  4.4 0.0 copy-start.5
  4.4 0.3 copy.24
  4.7 0.0 copy-done.2
  4.7 0.9 fusion
  5.6 0.0 copy-done.5
  5.6 1.2 fusion.2.n_ref
  6.8 0.0 copy-start.6
  6.9 0.0 copy-start.7
  6.9 0.0 copy-start.3
  6.9 0.0 copy-start.4
  6.9 0.0 copy-start.1
  6.9 111.4 %project.1 = (bf16[4,256,512]{2,1,0:T(8,128)(2,1)S(1)}, bf16[4,256,8192]{2,1,0:T(8,128)(2,1)S(1)}) custom-call(bf16[1024,512]{1,0:T(8,128)(2,1)S(1)} %bitcast.31, bf16[256,8192]{1,0:T(8,128)(2,1)S(1)} %fusion.2.n_ref), custom_call_target="tpu_custom_call" | custom-call | tf_op jit(solution)/shard_map/project/pallas_call | solution.py:212
  119.0 0.0 copy-done.6
  119.0 0.0 copy-done.7
  119.0 0.1 compare_and_fusion
  119.1 0.1 broadcast_compare_fusion
  119.9 0.0 copy-done.3
  119.9 0.0 copy-done.4
  120.0 0.0 copy-done.1
  120.0 22.7 %attention.1 = (bf16[128,1024]{1,0:T(8,128)(2,1)S(1)}, f32[128,1024]{1,0:T(8,128)S(1)}, f32[2,128,512]{2,1,0:T(8,128)S(1)}, bf16[2,512,512]{2,1,0:T(8,128)(2,1)S(1)}) custom-call(bf16[2,512,512]{2,1,0:T(8,128)(2,1)S(1)} %bitcast.34, bf16[128,1024]{1,0:T(8,128)(2,1)S(1)} %bitcast.37, bf16[2,128,512]{2,1,0:T(8,128)(2,1)S(1)} %bitcast.33, ...), custom_call_target="tpu_custom_call" | custom-call | tf_op jit(solution)/shard_map/attention/pallas_call | solution.py:296
  142.7 109.8 %scatter.1 = bf16[2,1024,512]{2,1,0:T(8,128)(2,1)S(1)} custom-call(bf16[1024,8192]{1,0:T(8,128)(2,1)S(1)} %bitcast.30, bf16[1024,512]{1,0:T(8,128)(2,1)S(1)} %bitcast.32), custom_call_target="tpu_custom_call" | custom-call | tf_op jit(solution)/shard_map/scatter/pallas_call | solution.py:390
  252.5 0.6 convert_bitcast_fusion
  253.1 5.3 %copy.20 = f32[1024,2,512]{2,1,0:T(2,128)} copy(f32[1024,2,512]{2,0,1:T(8,128)S(1)} %convert_bitcast_fusion) | data formatting | bytes 8388608
  258.4 1.2 copy.19
  259.6 0.7 copy.30
  260.3 0.8 copy.31
  (5 shorter events, 0.1 us)
Async XLA Ops:
  0.6 1.6 copy-start
  2.2 2.5 copy-start.2
  4.4 1.2 copy-start.5
  6.8 112.1 %copy-start.6 = (s32[1,128]{1,0:T(1,128)S(1)}, s32[1,128]{1,0:T(1,128)}, u32[]{:S(2)}) copy-start(s32[1,128]{1,0:T(1,128)} %param.17) | copy-start | bytes 1540
  6.9 112.1 %copy-start.7 = (s32[1,512]{1,0:T(1,128)S(1)}, s32[1,512]{1,0:T(1,128)}, u32[]{:S(2)}) copy-start(s32[1,512]{1,0:T(1,128)} %param.16) | copy-start | bytes 6148
  6.9 113.0 %copy-start.3 = (bf16[1,128,1024]{2,1,0:T(8,128)(2,1)S(1)}, bf16[1,128,1024]{2,1,0:T(8,128)(2,1)}, u32[]{:S(2)}) copy-start(bf16[1,128,1024]{2,1,0:T(8,128)(2,1)} %param.15) | copy-start | bytes 786436
  6.9 113.1 %copy-start.4 = (bf16[1,128,2,512]{3,2,1,0:T(2,128)(2,1)S(1)}, bf16[1,128,2,512]{3,2,1,0:T(2,128)(2,1)}, u32[]{:S(2)}) copy-start(bf16[1,128,2,512]{3,2,1,0:T(2,128)(2,1)} %param.14) | copy-start | bytes 786436
  6.9 113.1 %copy-start.1 = (bf16[1,128,1024]{2,1,0:T(8,128)(2,1)S(1)}, bf16[1,128,1024]{2,1,0:T(8,128)(2,1)}, u32[]{:S(2)}) copy-start(bf16[1,128,1024]{2,1,0:T(8,128)(2,1)} %param.13) | copy-start | bytes 786436

commit v4 on v2

--- a/solution.py
+++ b/solution.py
@@ -44,9 +44,10 @@
 
 
 def project_kernel(
-    ndp, nmp, w_ref, n_ref, kvc_ref, n_all, w_all, acc,
-    own_sem, zs, zr, xs, xr, ys, yr, ms, mr, fs, fr,
+    ndp, nmp, ns, w_ref, n_ref, *refs
 ):
+    given, (kvc_ref, n_all), taken, rest = refs[:ns], refs[ns : ns + 2], refs[ns + 2 : 2 * ns + 2], refs[2 * ns + 2 :]
+    w_all, acc, own_sem, zs, zr, xs, xr, ys, yr, ms, mr, fs, fr, ss, sr = rest
     nx = inner_of(ndp)
     nz = ndp // nx
     dp, seg, mp = lax.axis_index("dp"), lax.axis_index("segment"), lax.axis_index("mp")
@@ -99,6 +100,11 @@
         y_copy(o).start()
     for p in range(nmp - 1):
         m_copy(p).start()
+    swaps = [
+        remote(given[k].at[1 - seg], taken[k], ss.at[k], sr.at[k], y_peer) for k in range(ns)
+    ]
+    for copy in swaps:
+        copy.start()
     own_w.start()
     own_n.start()
     acc[...] = jnp.zeros_like(acc)
@@ -137,6 +143,8 @@
             finish(order[i - 1])
     finish(order[-1])
     kvc_ref[...] = acc[...].astype(kvc_ref.dtype)
+    for copy in swaps:
+        copy.wait()
     for o in order:
         if o > 0:
             for c in range(CHUNKS):
@@ -151,7 +159,7 @@
         m_copy(p).wait_send()
 
 
-def project(ndp, nseg, nmp, weight, normed):
+def project(ndp, nseg, nmp, weight, normed, given):
     nx = inner_of(ndp)
     nz = ndp // nx
     dma = pltpu.SemaphoreType.DMA
@@ -160,13 +168,14 @@
     cols = weight.shape[1]
     others, further = max(nmp - 1, 1), max(nz - 1, 1)
     return pl.pallas_call(
-        functools.partial(project_kernel, ndp, nmp),
+        functools.partial(project_kernel, ndp, nmp, len(given)),
         out_shape=(
             jax.ShapeDtypeStruct((nseg * nmp, rows, cols), jnp.bfloat16),
             jax.ShapeDtypeStruct((nseg * nmp, rows, width), normed.dtype),
-        ),
-        in_specs=[vmem, vmem],
-        out_specs=(vmem, vmem),
+        )
+        + tuple(jax.ShapeDtypeStruct(g.shape[1:], g.dtype) for g in given),
+        in_specs=[vmem] * (2 + len(given)),
+        out_specs=(vmem,) * (2 + len(given)),
         scratch_shapes=[
             pltpu.VMEM((ndp,) + weight.shape, weight.dtype),
             pltpu.VMEM((nseg * nmp, rows, cols), jnp.float32),
@@ -176,12 +185,13 @@
             dma((nz,)), dma((nz,)),
             dma((others,)), dma((others,)),
             dma((nz, others)), dma((nz, others)),
+            dma((max(len(given), 1),)), dma((max(len(given), 1),)),
         ],
         compiler_params=pltpu.CompilerParams(
             collective_id=0, has_side_effects=True, vmem_limit_bytes=20 * MiB
         ),
         name="project",
-    )(weight, normed)
+    )(weight, normed, *given)
 
 
 def attention_kernel(
@@ -265,7 +275,9 @@
     )(kvc, query, akv, grad_out, visible)
 
 
-def scatter_kernel(ndp, n_ref, g_ref, o_ref, x_send, x_buf, z_send, z_buf, xs, xr, zs, zr, ys, yr):
+def scatter_kernel(ndp, ns, n_ref, g_ref, *refs):
+    given, o_ref, whole, rest = refs[:ns], refs[ns], refs[ns + 1 : 2 * ns + 1], refs[2 * ns + 1 :]
+    x_send, x_buf, z_send, z_buf, xs, xr, zs, zr, ys, yr, ss = rest
     nx = inner_of(ndp)
     nz = ndp // nx
     dp, seg = lax.axis_index("dp"), lax.axis_index("segment")
@@ -296,6 +308,13 @@
 
     def y_copy(c):
         return remote(o_ref.at[seg, part(c)], o_ref.at[seg, part(c)], ys.at[c], yr.at[c], y_peer)
+
+    swaps = [
+        remote(given[k].at[1], whole[k].at[seg], ss.at[0, k], ss.at[1, k], y_peer) for k in range(ns)
+    ]
+    keeps = [pltpu.make_async_copy(given[k].at[0], whole[k].at[seg], ss.at[2, k]) for k in range(ns)]
+    for copy in swaps + keeps:
+        copy.start()
 
     if nx > 1:
         for o in order:
@@ -321,6 +340,9 @@
                 o_ref[seg, part(c), :] = total.astype(jnp.bfloat16)
                 y_copy(c).start()
 
+    for copy in swaps + keeps:
+        copy.wait()
+
     @pl.loop(0, steps)
     def _(c):
         y_copy(c).wait()
@@ -331,25 +353,134 @@
                 z_copy(o, c).wait_send()
 
 
-def scatter(ndp, nseg, tokens, grads):
+def scatter(ndp, nseg, tokens, grads, given):
     nx = inner_of(ndp)
     nz = ndp // nx
     dma = pltpu.SemaphoreType.DMA
     vmem = pl.BlockSpec(memory_space=pltpu.VMEM)
     block = (tokens.shape[1] // ndp, grads.shape[1])
     return pl.pallas_call(
-        functools.partial(scatter_kernel, ndp),
-        out_shape=jax.ShapeDtypeStruct((nseg,) + block, jnp.bfloat16),
-        in_specs=[vmem, vmem],
-        out_specs=vmem,
+        functools.partial(scatter_kernel, ndp, len(given)),
+        out_shape=(jax.ShapeDtypeStruct((nseg,) + block, jnp.bfloat16),)
+        + tuple(jax.ShapeDtypeStruct(g.shape, g.dtype) for g in given),
+        in_specs=[vmem] * (2 + len(given)),
+        out_specs=(vmem,) * (1 + len(given)),
         scratch_shapes=[pltpu.VMEM((nz,) + block, jnp.bfloat16)] * 4
         + [dma((nz, CHUNKS))] * 4
-        + [dma((CHUNKS,))] * 2,
+        + [dma((CHUNKS,))] * 2
+        + [dma((3, max(len(given), 1)))],
         compiler_params=pltpu.CompilerParams(
             collective_id=2, has_side_effects=True, vmem_limit_bytes=24 * MiB
         ),
         name="scatter",
-    )(tokens, grads)
+    )(tokens, grads, *given)
+
+
+def local_attention_kernel(heads, ratio, kvc, pack, code, pack_in, code_in, _, out_ref, dq_ref, dakv_ref, g_ref):
+    seg = lax.axis_index("segment")
+    acts = pack.shape[2]
+    rows = kvc.shape[1]
+    width = heads * HD
+    scale = HD ** (-0.5)
+
+    def dot(a, b, ca, cb):
+        return lax.dot_general(a, b, (((ca,), (cb,)), ((), ())), preferred_element_type=jnp.float32)
+
+    for t in range(2):
+        sample = seg if t == 0 else 1 - seg
+
+        def held(k, cols):
+            return pack[seg, k, :, cols] if t == 0 else pack_in[k, :, cols]
+
+        line = code[0, 0:1, :] if t == 0 else code_in[0:1, :]
+        level = jnp.broadcast_to(line[:, rows:], (acts, acts)).T
+        tiles = [
+            jnp.where(line[:, i * acts : (i + 1) * acts] <= level, 1.0, 0.0)
+            for i in range((rows + acts) // acts)
+        ]
+        visible = jnp.concatenate([jnp.concatenate(tiles, axis=1)] * ratio, axis=0) > 0.5
+        for g in range(heads):
+            kc, vc = slice(g * HD, (g + 1) * HD), slice(width + g * HD, width + (g + 1) * HD)
+            keys = jnp.concatenate([kvc[sample, :, kc], held(2, kc)], axis=0)
+            values = jnp.concatenate([kvc[sample, :, vc], held(2, vc)], axis=0)
+            hs = [slice((g * ratio + r) * HD, (g * ratio + r + 1) * HD) for r in range(ratio)]
+            query = jnp.concatenate([held(0, h) for h in hs], axis=0)
+            go = jnp.concatenate([held(1, h) for h in hs], axis=0)
+            masked = jnp.where(visible, dot(query, keys, 1, 1) * scale, NEGATIVE)
+            top = jnp.max(masked, axis=-1, keepdims=True)
+            expo = jnp.where(visible, jnp.exp(masked - top), 0.0)
+            probs = expo * (1.0 / jnp.sum(expo, axis=-1, keepdims=True))
+            low = probs.astype(jnp.bfloat16)
+            d_probs = dot(go, values, 1, 1)
+            delta = jnp.sum(probs * d_probs, axis=-1, keepdims=True)
+            d_scores = (probs * (d_probs - delta)).astype(jnp.bfloat16)
+            out = dot(low, values, 1, 0).astype(jnp.bfloat16)
+            d_query = dot(d_scores, keys, 1, 0) * scale
+            for r, h in enumerate(hs):
+                out_ref[t, :, h] = out[r * acts : (r + 1) * acts]
+                dq_ref[t, :, h] = d_query[r * acts : (r + 1) * acts]
+            d_keys = dot(d_scores, query, 0, 0) * scale
+            d_values = dot(low, go, 0, 0)
+            g_ref[sample, :, kc] = d_keys[:rows].astype(jnp.bfloat16)
+            g_ref[sample, :, vc] = d_values[:rows].astype(jnp.bfloat16)
+            dakv_ref[t, :, kc] = d_keys[rows:]
+            dakv_ref[t, :, vc] = d_values[rows:]
+
+
+def local_attention(heads, ratio, kvc, pack, code, pack_in, code_in, tokens):
+    vmem = pl.BlockSpec(memory_space=pltpu.VMEM)
+    nseg, _, acts, width = pack.shape
+    return pl.pallas_call(
+        functools.partial(local_attention_kernel, heads, ratio),
+        out_shape=(
+            jax.ShapeDtypeStruct((nseg, acts, width), jnp.bfloat16),
+            jax.ShapeDtypeStruct((nseg, acts, width), jnp.float32),
+            jax.ShapeDtypeStruct((nseg, acts, width), jnp.float32),
+            jax.ShapeDtypeStruct(kvc.shape, jnp.bfloat16),
+        ),
+        in_specs=[vmem] * 5 + [pl.BlockSpec(memory_space=pl.ANY)],
+        out_specs=(vmem,) * 4,
+        compiler_params=pltpu.CompilerParams(vmem_limit_bytes=8 * MiB),
+        name="local_attention",
+    )(kvc, pack, code, pack_in, code_in, tokens)
+
+
+def by_heads(ndp, nseg, nmp, weight, normed, query, akv, grad_out, pblocks, ablocks, length):
+    acts = query.shape[0]
+    depth, _, columns = weight.shape
+    part = columns // nseg
+    heads, ratio = part // HD, QH // KVH
+    rows = nmp * normed.shape[0]
+    width = normed.shape[1]
+    seg = lax.axis_index("segment")
+    own_weight = lax.dynamic_slice_in_dim(weight, seg * part, part, axis=2).reshape(depth, 2 * part)
+    pack = jnp.stack(
+        [
+            query.reshape(acts, nseg, 2 * part),
+            grad_out.reshape(acts, nseg, 2 * part),
+            akv.reshape(acts, 2, nseg, part).transpose(0, 2, 1, 3).reshape(acts, nseg, 2 * part),
+        ]
+    ).transpose(2, 0, 1, 3)
+    positions = jnp.arange(rows, dtype=jnp.int32)
+    seen_from = jnp.where(positions < length, pblocks.astype(jnp.float32), 1e9)
+    code = jnp.concatenate([seen_from, ablocks.astype(jnp.float32)])
+    code = jnp.broadcast_to(code, (nseg, 8, code.shape[0]))
+    kvc, tokens, pack_in, code_in = project(ndp, nseg, nmp, own_weight, normed, (pack, code))
+    out, d_query, d_action, grads = local_attention(
+        heads, ratio, kvc.reshape(nseg, rows, 2 * part), pack, code, pack_in, code_in, tokens
+    )
+    summed, out, d_query, d_action = scatter(
+        ndp,
+        nseg,
+        tokens.reshape(nseg * rows, width),
+        grads.reshape(nseg * rows, 2 * part),
+        (out, d_query, d_action),
+    )
+    attn_out = out.transpose(1, 0, 2).reshape(acts, nseg * 2 * part)
+    query_grad = d_query.transpose(1, 0, 2).reshape(acts, nseg * 2 * part)
+    d_action = d_action.reshape(nseg, acts, 2, part).transpose(1, 2, 0, 3).reshape(acts, 2, columns)
+    weight_grad = summed.reshape(nseg, depth, 2, part).transpose(1, 2, 0, 3).reshape(depth, 2, columns)
+    return (attn_out[None], query_grad[None], d_action[None], weight_grad.astype(jnp.float32))
 
 
 def shards(
@@ -374,13 +505,18 @@
     wide = prefix_hidden[0].astype(jnp.float32)
     inverse = lax.rsqrt(jnp.mean(wide * wide, axis=-1, keepdims=True) + EPS)
     normed_local = (wide * inverse * norm_gain).astype(jnp.bfloat16)
+    flow_weight = 0.5 + (timesteps[0].astype(jnp.float32) + 0.5) / STEPS
+    grad_out = (flow_weight * out_cotangent[0].astype(jnp.float32)).astype(jnp.bfloat16)
+    if ratio == 2 and heads_kv % nseg == 0:
+        return by_heads(
+            ndp, nseg, nmp, kv_weight, normed_local, action_query[0], action_kv[0], grad_out,
+            prefix_blocks[0], action_blocks[0], prefix_lengths[0],
+        )
     own_weight = lax.dynamic_index_in_dim(kv_weight, seg, axis=1, keepdims=False)
-    kvc, tokens = project(ndp, nseg, nmp, own_weight, normed_local)
+    kvc, tokens = project(ndp, nseg, nmp, own_weight, normed_local, ())
     rows = nmp * normed_local.shape[0]
     width = normed_local.shape[1]
     kvc = kvc.reshape(nseg, rows, columns)
-    flow_weight = 0.5 + (timesteps[0].astype(jnp.float32) + 0.5) / STEPS
-    grad_out = (flow_weight * out_cotangent[0].astype(jnp.float32)).astype(jnp.bfloat16)
     pblocks = prefix_blocks[0]
     ablocks = action_blocks[0]
     positions = jnp.arange(rows, dtype=jnp.int32)
@@ -390,8 +526,8 @@
     attn_out, query_grad, d_action, grads = attention(
         heads_kv, ratio, kvc, action_query[0], action_kv[0].transpose(1, 0, 2), grad_out, visible
     )
-    summed = scatter(
-        ndp, nseg, tokens.reshape(nseg * rows, width), grads.reshape(nseg * rows, columns)
+    (summed,) = scatter(
+        ndp, nseg, tokens.reshape(nseg * rows, width), grads.reshape(nseg * rows, columns), ()
     )
     weight_grad = summed.transpose(1, 0, 2).astype(jnp.float32)
     return (attn_out[None], query_grad[None], d_action.transpose(1, 0, 2)[None], weight_grad)

time: 258 us -> 261 us (1.012)
  local copies, waits for them, and re-layouts: 12 us -> 31.2 us
  Pallas kernels: 241 us -> 222 us
    pallas_call x3, Pallas kernels: 241 us -> 222 us  [the longest x1 112 us: scatter(): pl.pallas_call(functools.partial(scatter_kernel, ndp, len(given)), out_sh...]
    convert_element_type x0 -> x3, local copies, waits for them, and re-layouts: none -> 11.2 us  [the longest x2 11.1 us: by_heads(): weight_grad.astype(jnp.float32)]
    unnamed x22 -> x25, local copies, waits for them, and re-layouts: 9.89 us -> 14.6 us
where the time goes in v4:
time: 261 us
  Pallas kernels  222 us (85%)
  local copies, waits for them, and re-layouts  31.2 us (12%)
  other arithmetic  5.11 us (2%)
    pallas_call x1, Pallas kernels, scatter(): pl.pallas_call(functools.partial(scatter_kernel, ndp, len(given)), out_sh...  112 us
    pallas_call x1, Pallas kernels, project(): pl.pallas_call(functools.partial(project_kernel, ndp, nmp, len(given)), o...  107 us
    unnamed x25, local copies, waits for them, and re-layouts  14.6 us
    convert_element_type x2, local copies, waits for them, and re-layouts, by_heads(): weight_grad.astype(jnp.float32)  11.1 us

profile of v4, /device:TPU:0, one launch (start us, length us, event | category | flops | bytes accessed | tf_op | source)
XLA Modules:
  0.0 260.7 jit_solution(15994048153192511622)
XLA Ops:
  0.6 0.0 copy-start
  0.6 0.0 copy-start.9
  0.7 0.0 copy-start.7
  0.7 0.0 copy-start.6
  0.7 0.0 copy-start.5
  2.2 0.7 convert_bitcast_fusion
  2.8 3.1 %fusion = f32[256]{0:T(256)S(1)} fusion(bf16[1,256,8192]{2,1,0:T(8,128)(2,1)} %param.10), kind=kLoop, calls=%fused_computation.2 | loop fusion | flops 6291200 | bytes 4195328 | tf_op jit(solution)/shard_map/reduce_sum | solution.py:506
  6.0 0.0 copy-done.9
  6.0 0.0 copy-done.5
  6.0 0.2 copy.17
  6.2 0.2 copy.20
  6.4 0.0 copy-done.6
  6.4 0.2 reshape_squeeze.3
  6.5 0.0 copy-start.8
  6.6 0.2 copy.31
  6.8 0.2 stack_reshape.4
  6.9 0.0 copy-done.7
  7.0 0.2 copy.18
  7.1 0.1 multiply_convert_fusion
  7.2 0.1 copy.21
  7.4 0.0 copy-start.4
  7.4 0.1 maximum_bitcast_fusion.refs_0_.pack
  7.5 0.0 copy-done
  7.5 0.7 constant_dynamic-slice_fusion
  8.2 0.2 copy.29
  8.5 0.0 copy-done.8
  8.5 1.1 copy-done.4
  9.5 1.2 fusion.2.n_ref
  10.7 106.6 %project.1 = (bf16[4,256,512]{2,1,0:T(8,128)(2,1)S(1)}, bf16[4,256,8192]{2,1,0:T(8,128)(2,1)S(1)}, bf16[3,128,512]{2,1,0:T(8,128)(2,1)S(1)}, f32[8,640]{1,0:T(8,128)S(1)}) custom-call(bf16[1024,512]{1,0:T(8,128)(2,1)S(1)} %bitcast.33, bf16[256,8192]{1,0:T(8,128)(2,1)S(1)} %fusion.2.n_ref, bf16[2,3,128,512]{3,2,1,0:T(8,128)(2,1)S(1)} %maximum_bitcast_fusion.refs_0_.pack, ...), custom_call_target="tpu_custom_call" | custom-call | tf_op jit(solution)/shard_map/project/pallas_call | solution.py:170
  117.3 0.0 copy-start.1
  117.3 3.8 %local_attention.1 = (bf16[2,128,512]{2,1,0:T(8,128)(2,1)S(1)}, f32[2,128,512]{2,1,0:T(8,128)S(1)}, f32[2,128,512]{2,1,0:T(8,128)S(1)}, bf16[2,512,512]{2,1,0:T(8,128)(2,1)S(1)}) custom-call(bf16[2,512,512]{2,1,0:T(8,128)(2,1)S(1)} %bitcast.35, bf16[2,3,128,512]{3,2,1,0:T(8,128)(2,1)S(1)} %maximum_bitcast_fusion.refs_0_.pack, ...), custom_call_target="tpu_custom_call" | custom-call | tf_op jit(solution)/shard_map/local_attention/pallas_call | solution.py:433
  121.1 2.0 copy-done.1
  123.1 0.0 copy-start.2
  123.1 5.8 %copy-done.2 = bf16[4,256,8192]{2,1,0:T(8,128)(2,1)S(1)} copy-done((bf16[4,256,8192]{2,1,0:T(8,128)(2,1)S(1)}, bf16[4,256,8192]{2,1,0:T(8,128)(2,1)}, u32[]{:S(2)}) %copy-start.2) | copy-done | bytes 16777240
  128.8 111.6 %scatter.1 = (bf16[2,1024,512]{2,1,0:T(8,128)(2,1)S(1)}, bf16[2,128,512]{2,1,0:T(8,128)(2,1)S(1)}, f32[2,128,512]{2,1,0:T(8,128)S(1)}, f32[2,128,512]{2,1,0:T(8,128)S(1)}) custom-call(bf16[1024,8192]{1,0:T(8,128)(2,1)S(1)} %bitcast.32, bf16[1024,512]{1,0:T(8,128)(2,1)S(1)} %bitcast.34, bf16[2,128,512]{2,1,0:T(8,128)(2,1)S(1)} %get-tuple-element.21.refs_0_, ...), custom_call_target="tpu_custom_call" | custom-call | tf_op jit(solution)/shard_map/scatter/pallas_call | solution.py:362
  240.5 0.0 copy-start.3
  240.5 1.3 copy-done.3
  241.8 0.8 copy.22
  242.6 1.8 copy.26
  244.4 1.0 copy.23
  245.4 2.0 copy.27
  247.5 0.3 reshape.73
  247.8 0.4 copy.24
  248.2 1.4 broadcast_in_dim_reshape.11
  249.6 5.4 %reshape.76 = f32[2,1024,2,256]{3,2,1,0:T(2,128)} reshape(bf16[2,1024,512]{2,1,0:T(8,128)(2,1)} %copy-done.3) | data formatting | bytes 6291456 | tf_op jit(solution)/shard_map/convert_element_type | solution.py:483
  255.0 5.6 %copy.28 = f32[2,1024,1,2,256]{4,3,0,2,1:T(2,128)} copy(f32[2,1024,1,2,256]{4,3,2,1,0:T(2,128)} %bitcast.38) | data formatting | bytes 8388608 | tf_op jit(solution)/shard_map/convert_element_type | solution.py:483
  (5 shorter events, 0.0 us)
Async XLA Ops:
  0.6 6.8 %copy-start = (bf16[1024,2,512]{2,1,0:T(2,128)(2,1)S(1)}, bf16[1024,2,512]{2,1,0:T(2,128)(2,1)}, u32[]{:S(2)}) copy-start(bf16[1024,2,512]{2,1,0:T(2,128)(2,1)} %param.12) | copy-start | bytes 6291460
  0.6 5.3 %copy-start.9 = (s32[1,512]{1,0:T(1,128)S(1)}, s32[1,512]{1,0:T(1,128)}, u32[]{:S(2)}) copy-start(s32[1,512]{1,0:T(1,128)} %param.16) | copy-start | bytes 6148
  0.7 6.3 %copy-start.7 = (bf16[1,128,1024]{2,1,0:T(8,128)(2,1)S(1)}, bf16[1,128,1024]{2,1,0:T(8,128)(2,1)}, u32[]{:S(2)}) copy-start(bf16[1,128,1024]{2,1,0:T(8,128)(2,1)} %param.15) | copy-start | bytes 786436
  0.7 5.7 %copy-start.6 = (bf16[1,128,2,512]{3,2,1,0:T(2,128)(2,1)S(1)}, bf16[1,128,2,512]{3,2,1,0:T(2,128)(2,1)}, u32[]{:S(2)}) copy-start(bf16[1,128,2,512]{3,2,1,0:T(2,128)(2,1)} %param.14) | copy-start | bytes 786436
  0.7 5.3 %copy-start.5 = (bf16[1,128,1024]{2,1,0:T(8,128)(2,1)S(1)}, bf16[1,128,1024]{2,1,0:T(8,128)(2,1)}, u32[]{:S(2)}) copy-start(bf16[1,128,1024]{2,1,0:T(8,128)(2,1)} %param.13) | copy-start | bytes 786436
  6.5 1.9 copy-start.8
  7.4 2.2 copy-start.4
  117.3 5.7 %copy-start.1 = (bf16[4,256,8192]{2,1,0:T(8,128)(2,1)}, bf16[4,256,8192]{2,1,0:T(8,128)(2,1)S(1)}, u32[]{:S(2)}) copy-start(bf16[4,256,8192]{2,1,0:T(8,128)(2,1)S(1)} %get-tuple-element.16._) | copy-start | bytes 50331652
  123.1 5.8 %copy-start.2 = (bf16[4,256,8192]{2,1,0:T(8,128)(2,1)S(1)}, bf16[4,256,8192]{2,1,0:T(8,128)(2,1)}, u32[]{:S(2)}) copy-start(bf16[4,256,8192]{2,1,0:T(8,128)(2,1)} %copy-done.1) | copy-start | bytes 50331652
  240.5 1.3 copy-start.3
